TPU v7x, 32 devices: a whole 2x2x4 slice. The times are simulated.
32 devices in a mesh: group: 2 (over x), ccd: 16 (over z, y, core).
Axes of the slice: x: 2, y: 2, z: 4, core: 2. Of those that a mesh axis runs over, the one named last changes fastest.
Arguments:
- images: float32 [4, 4096, 512], P(None, ('group', 'ccd')), parts along dimension 1, may hold values from -6 to 6
- basis_taps: float32 [2, 9, 11], replicated, may hold values from -1.75 to 1.75
- psf_coef: float32 [4, 10, 9, 3], P(None, 'group'), parts along dimension 1, may hold values from -3 to 3
- affine: float32 [4, 10, 2, 2], P(None, 'group'), parts along dimension 1, may hold values from -0.5 to 0.5
- visit_weight: bfloat16 [4, 10], P(None, 'group'), parts along dimension 1, may hold values from 0.25 to 4
- block_patch: int32 [32, 16, 1], P(('group', 'ccd')), parts along dimension 0, may hold values from 0 to 15; in each aligned block of 16 rows (0 to 15, 16 to 31, ..., all dimensions but the last counted through in order) at most 2 rows name the same one
- block_slot: int32 [32, 16], P(('group', 'ccd')), parts along dimension 0, may hold values from 0 to 15
- patch_owner: int32 [32], P('group'), parts along dimension 0, may hold values from 0 to 15, each once
Outputs:
- coadd: float32 [32, 512, 512], P(('group', 'ccd')), parts along dimension 0
There are 2 independent parts, one for each index of `group`. A program takes and returns all parts, laid end to end along the dimension named above; an argument that names none is the same for every part. Nothing has to cross between parts.
Inputs may be any that keep to these rules, and one draw needn't show every extreme that they name: `block_patch`: among the 16 blocks of one band no patch is named more than 2 times, and in every draw some band names some patch exactly 2 times. `patch_owner`: each device index along ccd owns exactly one patch.
All inputs are finite; a program needn't handle non-finite values.
Results may differ from a plain program's by a relative error of at most 0.0029.
Values may be sent and summed in bfloat16 or wider, within the bound.
A program may use at most 64 MiB of HBM per device.

v0:
```python
import functools

import jax
import jax.numpy as jnp
from jax import lax
from jax.experimental import pallas as pl
from jax.experimental.pallas import tpu as pltpu
from jax.sharding import PartitionSpec as P

V = 4
BLOCK = 128
BLKC = 4
SPLIT = 4
TAPS = 11
NBASIS = 9
PSIDE = 4
HALF = TAPS // 2
REACH = 3
RIM = HALF + REACH
CHUNKS = 2
CHUNK = BLOCK // CHUNKS
ROWS_IN = CHUNK + 2 * RIM
ROWS_MID = CHUNK + 8
WIDTH = BLKC * BLOCK
HEIGHT = SPLIT * BLOCK
LEFT = BLOCK // 2
STEPS = 2 * REACH + 1


def sinc(values):
    angle = jnp.pi * values
    zero = values == 0.0
    return jnp.where(zero, 1.0, jnp.sin(angle) / jnp.where(zero, 1.0, angle))


def lanczos(offset):
    inside = jnp.abs(offset) < 3.0
    return jnp.where(inside, sinc(offset) * sinc(offset / 3.0), 0.0)


def outward(count):
    far = sorted(range(1, count), key=lambda step: abs(step - count // 2))
    half = len(far) // 2
    near = far[half:][::-1]
    mixed = [step for pair in zip(far[:half], near) for step in pair]
    return mixed + near[half:]


def rim_kernel(count, image_ref, above_ref, below_ref, rims):
    me = lax.axis_index("ccd")
    barrier = pltpu.get_barrier_semaphore()
    has_next, has_last = me < count - 1, me > 0

    def to_next():
        return pltpu.make_async_remote_copy(
            src_ref=image_ref.at[:, pl.ds(BLOCK - RIM, RIM)],
            dst_ref=above_ref,
            send_sem=rims.at[0],
            recv_sem=rims.at[1],
            device_id={"ccd": lax.rem(me + 1, count)},
            device_id_type=pl.DeviceIdType.MESH,
        )

    def to_last():
        return pltpu.make_async_remote_copy(
            src_ref=image_ref.at[:, pl.ds(0, RIM)],
            dst_ref=below_ref,
            send_sem=rims.at[2],
            recv_sem=rims.at[3],
            device_id={"ccd": lax.rem(me + count - 1, count)},
            device_id_type=pl.DeviceIdType.MESH,
        )

    for present, step in ((has_next, 1), (has_last, count - 1)):

        @pl.when(present)
        def _(step=step):
            pl.semaphore_signal(
                barrier,
                inc=1,
                device_id={"ccd": lax.rem(me + step, count)},
                device_id_type=pl.DeviceIdType.MESH,
            )

    pl.semaphore_wait(barrier, has_next.astype(jnp.int32) + has_last.astype(jnp.int32))

    @pl.when(has_next)
    def _():
        to_next().start()

    @pl.when(has_last)
    def _():
        to_last().start()

    @pl.when(has_next)
    def _():
        to_next().wait_send()
        to_last().wait_recv()

    @pl.when(has_last)
    def _():
        to_last().wait_send()
        to_next().wait_recv()


def split(values):
    high = values.astype(jnp.bfloat16)
    return high, (values - high.astype(jnp.float32)).astype(jnp.bfloat16)


def dot(left, right):
    return jnp.dot(left, right, preferred_element_type=jnp.float32)


def plan_kernel(devices, capacity, patch_ref, slot_ref, owner_ref, block_ref, meta_ref, filled):
    for device in range(devices):
        filled[device] = 0
    for slot in range(devices * capacity):
        block_ref[slot] = 0
    lane = lax.broadcasted_iota(jnp.int32, meta_ref.shape, 1)
    meta = jnp.zeros(meta_ref.shape, jnp.int32)
    for block in range(V * BLKC):
        patch = patch_ref[block]
        meta = jnp.where(lane == block, patch, meta)
        meta = jnp.where(lane == V * BLKC + block, slot_ref[0, block], meta)
        device = owner_ref[patch]
        block_ref[device * capacity + filled[device]] = block
        filled[device] = filled[device] + 1
    meta_ref[...] = meta


def band_kernel(
    devices,
    capacity,
    block_ref,
    taps_ref,
    coef_ref,
    affine_ref,
    meta_ref,
    above_ref,
    image_ref,
    below_ref,
    metas_ref,
    got_ref,
    col_high,
    col_low,
    row_kernel,
    wide,
    terms_high,
    terms_low,
    mid,
    stage,
    outbox,
    sent,
    received,
    own,
):
    band = lax.axis_index("ccd")
    barrier = pltpu.get_barrier_semaphore()
    for step in range(1, devices):
        pl.semaphore_signal(
            barrier,
            inc=1,
            device_id={"ccd": lax.rem(band + step, devices)},
            device_id_type=pl.DeviceIdType.MESH,
        )
    shifted = band + SPLIT // 2
    ccd = shifted // SPLIT
    top_row = shifted % SPLIT * BLOCK
    region_shift = band * BLOCK - top_row
    region_low = jnp.maximum(0, -region_shift)
    region_high = jnp.minimum(HEIGHT, devices * BLOCK - region_shift)
    ccds = coef_ref.shape[0] // (V * NBASIS * 3)
    wide_lane = lax.broadcasted_iota(jnp.int32, (1, NBASIS * ROWS_IN), 1)

    def by_basis(value):
        total = jnp.full((1, NBASIS * ROWS_IN), value(0), jnp.float32)
        for basis in range(1, NBASIS):
            total = jnp.where(wide_lane >= basis * ROWS_IN, value(basis), total)
        return total

    def inside(first, count):
        rows = first + lax.broadcasted_iota(jnp.int32, (count, 1), 0)
        return (rows >= region_low) & (rows < region_high)

    depth = lax.broadcasted_iota(jnp.int32, (2 * BLOCK, BLOCK), 0)
    lane = lax.broadcasted_iota(jnp.int32, (2 * BLOCK, BLOCK), 1)
    distance = depth - (LEFT - HALF) - lane
    for basis in range(NBASIS):
        cols = pl.ds(basis * BLOCK, BLOCK)
        total = jnp.zeros((2 * BLOCK, BLOCK), jnp.float32)
        for tap in range(TAPS):
            total = jnp.where(
                distance == tap, taps_ref[1, basis, tap], total
            )
        high, low = split(total)
        col_high[:, cols] = high
        col_low[:, cols] = low
    start = jnp.zeros((1, NBASIS * ROWS_IN), jnp.int32)
    for basis in range(1, NBASIS):
        start = jnp.where(wide_lane >= basis * ROWS_IN, basis * ROWS_IN, start)
    gap = (wide_lane - start) - lax.broadcasted_iota(
        jnp.int32, (ROWS_MID, NBASIS * ROWS_IN), 0
    )
    total = jnp.zeros(gap.shape, jnp.float32)
    for tap in range(TAPS):
        total = jnp.where(
            gap == tap, by_basis(lambda basis: taps_ref[0, basis, tap]), total
        )
    row_kernel[...] = total
    wide[...] = jnp.zeros_like(wide)

    column = lax.broadcasted_iota(jnp.int32, (1, WIDTH), 1).astype(jnp.float32)
    col_pos = (2.0 * column + 1.0) / WIDTH - 1.0

    def remote(source, target, kind, step):
        return pltpu.make_async_remote_copy(
            src_ref=source,
            dst_ref=target,
            send_sem=sent.at[kind, step],
            recv_sem=received.at[kind, step],
            device_id={"ccd": lax.rem(band + step, devices)},
            device_id_type=pl.DeviceIdType.MESH,
        )

    pl.semaphore_wait(barrier, devices - 1)
    copies = [
        remote(meta_ref, metas_ref.at[band], CHUNKS, step) for step in outward(devices)
    ]
    locals_ = [pltpu.make_async_copy(meta_ref, metas_ref.at[band], own.at[CHUNKS])]
    for copy in copies + locals_:
        copy.start()
    for chunk in range(CHUNKS):
        first = top_row + chunk * CHUNK

        def one_visit(visit, carry, chunk=chunk, first=first):
            place = visit * ccds + ccd
            raw = jnp.concatenate([above_ref[visit], image_ref[visit], below_ref[visit]], axis=0)
            raw = raw[chunk * CHUNK : chunk * CHUNK + ROWS_IN]
            raw = jnp.where(inside(first - RIM, ROWS_IN), raw, 0.0)
            wide[:, LEFT : LEFT + WIDTH] = raw
            for block in range(BLKC):
                high, low = split(wide[:, block * BLOCK : (block + 2) * BLOCK])
                term = dot(high, col_high[...]) + dot(low, col_high[...]) + dot(high, col_low[...])
                high, low = split(term)
                for basis in range(NBASIS):
                    rows = pl.ds(basis * ROWS_IN, ROWS_IN)
                    cols = pl.ds(block * BLOCK, BLOCK)
                    terms_high[rows, cols] = high[:, basis * BLOCK : (basis + 1) * BLOCK]
                    terms_low[rows, cols] = low[:, basis * BLOCK : (basis + 1) * BLOCK]

            position = (first - REACH + lax.broadcasted_iota(jnp.int32, (ROWS_MID, 1), 0)).astype(
                jnp.float32
            )
            row_pos = (2.0 * position + 1.0) / HEIGHT - 1.0
            kernel = row_kernel[...]
            constant, by_row, by_column = (
                by_basis(lambda basis: coef_ref[(place * NBASIS + basis) * 3 + part]) for part in range(3)
            )
            level = kernel * (constant + by_row * row_pos)
            slope = kernel * by_column
            level_high, level_low = split(level)
            slope_high, slope_low = split(slope)
            upper = dot(
                jnp.concatenate([level_high, slope_high, level_low, slope_low], axis=0), terms_high[...]
            )
            lower = dot(jnp.concatenate([level_high, slope_high], axis=0), terms_low[...])
            both = upper[: 2 * ROWS_MID] + upper[2 * ROWS_MID :] + lower
            matched = both[:ROWS_MID] + both[ROWS_MID:] * col_pos
            mid[...] = jnp.where(inside(first - REACH, ROWS_MID), matched, 0.0)

            own_rows = (first + lax.broadcasted_iota(jnp.int32, (CHUNK, 1), 0)).astype(jnp.float32)
            row_shift = affine_ref[visit, ccd, 0, 0] + affine_ref[visit, ccd, 0, 1] * (
                (own_rows - (HEIGHT - 1) / 2.0) / HEIGHT
            )
            row_step = lax.broadcasted_iota(jnp.int32, (CHUNK, BLOCK), 1) - REACH
            row_weight = lanczos(row_shift - row_step.astype(jnp.float32))
            col_shift = affine_ref[visit, ccd, 1, 0] + affine_ref[visit, ccd, 1, 1] * (
                (column - (WIDTH - 1) / 2.0) / WIDTH
            )
            col_step = lax.broadcasted_iota(jnp.int32, (8, WIDTH), 0) - REACH
            reached = lax.broadcasted_iota(jnp.int32, (8, WIDTH), 1) + col_step
            col_weight = jnp.where(
                (reached >= 0) & (reached < WIDTH),
                lanczos(col_shift - col_step.astype(jnp.float32)),
                0.0,
            )
            warped = jnp.zeros((CHUNK, WIDTH), jnp.float32)
            for step in range(STEPS):
                warped = warped + row_weight[:, step : step + 1] * mid[step : step + CHUNK, :]
            total = jnp.zeros((CHUNK, WIDTH), jnp.float32)
            for step in range(STEPS):
                offset = step - REACH
                moved = warped if offset == 0 else pltpu.roll(warped, (-offset) % WIDTH, 1)
                total = total + col_weight[step : step + 1, :] * moved
            rounded = total.astype(jnp.bfloat16)
            for block in range(BLKC):
                stage[chunk * V * BLKC + visit * BLKC + block] = rounded[
                    :, block * BLOCK : (block + 1) * BLOCK
                ]
            return carry

        lax.fori_loop(0, V, one_visit, 0)
        for device in range(devices):
            for slot in range(capacity):
                outbox[chunk, device, slot] = stage[
                    chunk * V * BLKC + block_ref[device * capacity + slot]
                ]
        batch = [
            remote(
                outbox.at[chunk, lax.rem(band + step, devices)],
                got_ref.at[chunk, band],
                chunk,
                step,
            )
            for step in outward(devices)
        ]
        local = pltpu.make_async_copy(
            outbox.at[chunk, band], got_ref.at[chunk, band], own.at[chunk]
        )
        for copy in batch + [local]:
            copy.start()
        copies += batch
        locals_.append(local)
    for copy in locals_ + copies:
        copy.wait()


def gather_kernel(devices, capacity, meta_ref, owner_ref, weight_ref, got_ref, out_ref, total, weights):
    me = lax.axis_index("ccd")
    total[...] = jnp.zeros_like(total)
    for cell in range(PSIDE * PSIDE):
        weights[cell] = 0.0
    patch = jnp.int32(0)
    for candidate in range(owner_ref.shape[0]):
        patch = jnp.where(owner_ref[candidate] == me, candidate, patch)
    count = V * BLKC

    def add(source, carry):
        ccd = (source + SPLIT // 2) // SPLIT
        taken = source * capacity
        for block in range(count):
            mine = meta_ref[source, 0, block] == patch

            @pl.when(mine)
            def _(taken=taken, block=block):
                cell = meta_ref[source, 0, count + block]
                weight = weight_ref[block // BLKC, ccd]
                weights[cell] = weights[cell] + weight
                for chunk in range(CHUNKS):
                    rows = pl.ds(chunk * CHUNK, CHUNK)
                    total[cell, rows] = total[cell, rows] + weight * got_ref[
                        chunk, taken
                    ].astype(jnp.float32)

            taken = taken + mine.astype(jnp.int32)
        return carry

    lax.fori_loop(0, devices, add, 0)
    for cell in range(PSIDE * PSIDE):
        row, col = cell // PSIDE * BLOCK, cell % PSIDE * BLOCK
        scale = jnp.full((1, BLOCK), jnp.maximum(weights[cell], 1.0), jnp.float32)
        out_ref[0, row : row + BLOCK, col : col + BLOCK] = total[cell] / scale


def shards(
    images, basis_taps, psf_coef, affine, visit_weight, block_patch, block_slot, patch_owner
):
    devices = lax.axis_size("ccd")
    block_count = V * BLKC
    capacity = max(2, (2 * block_count + devices - 1) // devices)
    slots = devices * capacity
    anywhere = pl.BlockSpec(memory_space=pl.ANY)
    scalars = pl.BlockSpec(memory_space=pltpu.SMEM)
    vector = pl.BlockSpec(memory_space=pltpu.VMEM)
    lanes = -(-2 * block_count // BLOCK) * BLOCK
    rim_shape = jax.ShapeDtypeStruct((V, RIM, WIDTH), jnp.float32)
    above, below = pl.pallas_call(
        functools.partial(rim_kernel, devices),
        out_shape=(rim_shape, rim_shape),
        in_specs=[anywhere],
        out_specs=(anywhere, anywhere),
        scratch_shapes=[pltpu.SemaphoreType.DMA((4,))],
        compiler_params=pltpu.CompilerParams(collective_id=1, has_side_effects=True),
    )(images)

    blocks, meta = pl.pallas_call(
        functools.partial(plan_kernel, devices, capacity),
        out_shape=(
            jax.ShapeDtypeStruct((slots,), jnp.int32),
            jax.ShapeDtypeStruct((1, lanes), jnp.int32),
        ),
        in_specs=[scalars] * 3,
        out_specs=(scalars, vector),
        scratch_shapes=[pltpu.SMEM((devices,), jnp.int32)],
    )(block_patch.reshape(-1), block_slot, patch_owner)
    metas, got = pl.pallas_call(
        functools.partial(band_kernel, devices, capacity),
        out_shape=(
            jax.ShapeDtypeStruct((devices, 1, lanes), jnp.int32),
            jax.ShapeDtypeStruct((CHUNKS, devices, capacity, CHUNK, BLOCK), jnp.bfloat16),
        ),
        in_specs=[scalars] * 4 + [vector] * 4,
        out_specs=(vector, anywhere),
        scratch_shapes=[
            pltpu.VMEM((2 * BLOCK, NBASIS * BLOCK), jnp.bfloat16),
            pltpu.VMEM((2 * BLOCK, NBASIS * BLOCK), jnp.bfloat16),
            pltpu.VMEM((ROWS_MID, NBASIS * ROWS_IN), jnp.float32),
            pltpu.VMEM((ROWS_IN, WIDTH + BLOCK), jnp.float32),
            pltpu.VMEM((NBASIS * ROWS_IN, WIDTH), jnp.bfloat16),
            pltpu.VMEM((NBASIS * ROWS_IN, WIDTH), jnp.bfloat16),
            pltpu.VMEM((ROWS_MID, WIDTH), jnp.float32),
            pltpu.VMEM((CHUNKS * block_count, CHUNK, BLOCK), jnp.bfloat16),
            pltpu.VMEM((CHUNKS, devices, capacity, CHUNK, BLOCK), jnp.bfloat16),
            pltpu.SemaphoreType.DMA((CHUNKS + 1, devices)),
            pltpu.SemaphoreType.DMA((CHUNKS + 1, devices)),
            pltpu.SemaphoreType.DMA((CHUNKS + 1,)),
        ],
        compiler_params=pltpu.CompilerParams(collective_id=2, has_side_effects=True),
    )(
        blocks,
        basis_taps,
        psf_coef.reshape(-1),
        affine,
        meta,
        above,
        images,
        below,
    )
    size = PSIDE * BLOCK
    return pl.pallas_call(
        functools.partial(gather_kernel, devices, capacity),
        out_shape=jax.ShapeDtypeStruct((1, size, size), jnp.float32),
        in_specs=[scalars, scalars, scalars, vector],
        out_specs=vector,
        scratch_shapes=[
            pltpu.VMEM((PSIDE * PSIDE, BLOCK, BLOCK), jnp.float32),
            pltpu.SMEM((PSIDE * PSIDE,), jnp.float32),
        ],
    )(metas, patch_owner, visit_weight.astype(jnp.float32), got.reshape(CHUNKS, slots, CHUNK, BLOCK))


def solution(mesh):
    placed = (
        P(None, ("group", "ccd"), None),
        P(),
        P(None, "group", None, None),
        P(None, "group", None, None),
        P(None, "group"),
        P(("group", "ccd"), None, None),
        P(("group", "ccd"), None),
        P("group"),
    )
    return jax.shard_map(
        shards,
        mesh=mesh,
        in_specs=placed,
        out_specs=P(("group", "ccd"), None, None),
        check_vma=False,
    )
```

profile of v0, /device:TPU:0, one launch (start us, length us, event | category | flops | bytes accessed | tf_op | source)
XLA Modules:
  0.0 55.4 jit_solution(11422513502979667823)
XLA Ops:
  0.0 0.0 copy-start.1
  0.0 1.4 %shard_map.82 = (s32[32]{0:T(128)}, s32[1,128]{1,0:T(1,128)}) custom-call(s32[16]{0:T(128)} %bitcast.3, s32[1,16]{1,0:T(1,128)} %slot_ref.1, s32[16]{0:T(128)} %owner_ref.3), custom_call_target="tpu_custom_call" | custom-call | tf_op jit(solution)/shard_map/pallas_call | solution.py:387
  1.4 1.3 %convert_element_type.3.weight_ref = f32[4,5]{1,0:T(4,128)} convert(bf16[4,5]{1,0:T(4,128)(2,1)} %param.12) | non-fusion elementwise | flops 20 | bytes 120 | tf_op jit(solution)/shard_map/convert_element_type | solution.py:440
  2.7 0.0 copy-done.1
  2.7 0.0 copy-start.2
  2.7 0.6 %copy.12.taps_ref = f32[2,9,11]{2,1,0:T(8,128)} copy(f32[2,9,11]{2,0,1:T(2,128)S(1)} %copy-done.1) | data formatting | bytes 1584 | tf_op args[1]
  3.3 0.1 copy-done.2
  3.4 0.7 %copy.13.affine_ref = f32[4,5,2,2]{3,2,1,0:T(2,128)} copy(f32[4,5,2,2]{1,3,2,0:T(2,128)S(1)} %copy-done.2) | data formatting | bytes 640 | tf_op args[3]
  4.2 0.0 copy-start
  4.2 4.2 %shard_map.83 = (f32[4,8,512]{2,1,0:T(8,128)}, f32[4,8,512]{2,1,0:T(8,128)}) custom-call(f32[4,128,512]{2,1,0:T(8,128)} %image_ref.3), custom_call_target="tpu_custom_call" | custom-call | tf_op jit(solution)/shard_map/pallas_call | solution.py:378
  8.4 0.0 copy-done
  8.4 0.2 copy.11
  8.6 0.8 %reshape.10.coef_ref = f32[540]{0:T(1024)} reshape(f32[4,5,9,3]{3,2,1,0:T(8,128)S(1)} %copy.11) | data formatting | bytes 4320 | tf_op jit(solution)/shard_map/reshape | solution.py:423
  9.4 40.9 %shard_map.84 = (s32[16,1,128]{2,1,0:T(1,128)}, bf16[2,16,2,64,128]{4,3,2,1,0:T(8,128)(2,1)}) custom-call(s32[32]{0:T(128)} %get-tuple-element.11.block_ref, f32[2,9,11]{2,1,0:T(8,128)} %copy.12.taps_ref, f32[540]{0:T(1024)} %reshape.10.coef_ref, f32[4,5,2,2]{3,2,1,0:T(2,128)} %copy.13.affine_ref, s32[1,128]{1,0:T(1,128)} %get-tuple-element.12.meta_ref, ...), custom_call_target="tpu_custom_call" | custom-call | tf_op jit(solution)/shard_map/pallas_call | solution.py:397
  50.3 5.1 %shard_map.85 = f32[1,512,512]{2,1,0:T(8,128)} custom-call(s32[16,1,128]{2,1,0:T(1,128)} %get-tuple-element.15.meta_ref, s32[16]{0:T(128)} %owner_ref.3, f32[4,5]{1,0:T(4,128)} %convert_element_type.3.weight_ref, bf16[2,32,64,128]{3,2,1,0:T(8,128)(2,1)} %bitcast.2), custom_call_target="tpu_custom_call" | custom-call | tf_op jit(solution)/shard_map/pallas_call | solution.py:431
Async XLA Ops:
  0.0 2.7 %copy-start.1 = (f32[2,9,11]{2,0,1:T(2,128)S(1)}, f32[2,9,11]{2,0,1:T(2,128)}, u32[]{:S(2)}) copy-start(f32[2,9,11]{2,0,1:T(2,128)} %param.9) | copy-start | bytes 2380
  2.7 0.7 %copy-start.2 = (f32[4,5,2,2]{1,3,2,0:T(2,128)S(1)}, f32[4,5,2,2]{1,3,2,0:T(2,128)}, u32[]{:S(2)}) copy-start(f32[4,5,2,2]{1,3,2,0:T(2,128)} %param.11) | copy-start | bytes 964
  4.2 4.2 %copy-start = (f32[4,5,9,3]{2,0,3,1:T(4,128)S(1)}, f32[4,5,9,3]{2,0,3,1:T(4,128)}, u32[]{:S(2)}) copy-start(f32[4,5,9,3]{2,0,3,1:T(4,128)} %param.10) | copy-start | bytes 6484
where the time goes:
time: 55.7 us; the launch traced here: 55.4 us
  Pallas kernels  51.6 us (93%)
  local copies, waits for them, and re-layouts  2.47 us (4%)
  other arithmetic  1.26 us (2%)
    pallas_call x1, Pallas kernels, shards(): pl.pallas_call(functools.partial(band_kernel, devices, capacity), out_sha...  40.9 us
    pallas_call x1, Pallas kernels, shards(): pl.pallas_call(functools.partial(gather_kernel, devices, capacity), out_s...  5.07 us
    pallas_call x1, Pallas kernels, shards(): pl.pallas_call(functools.partial(rim_kernel, devices), out_shape=(rim_sha...  4.23 us
    unnamed x9, local copies, waits for them, and re-layouts  1.68 us
    pallas_call x1, Pallas kernels, shards(): pl.pallas_call(functools.partial(plan_kernel, devices, capacity), out_sha...  1.44 us
    convert_element_type x1, other arithmetic, shards(): visit_weight.astype(jnp.float32)  1.26 us

commit v1 on v0

v1 whole, which is shorter than its diff:
```python
import functools
import math

import jax
import jax.numpy as jnp
from jax import lax
from jax.experimental import pallas as pl
from jax.experimental.pallas import tpu as pltpu
from jax.sharding import PartitionSpec as P

V = 4
BLOCK = 128
BLKC = 4
SPLIT = 4
TAPS = 11
NBASIS = 9
PSIDE = 4
CELLS = PSIDE * PSIDE
HALF = TAPS // 2
REACH = 3
RIM = HALF + REACH
CHUNK = 32
ORDER = (1, 2, 0, 3)
EXT = BLOCK + 2 * RIM
ROWS_IN = CHUNK + 2 * RIM
ROWS_MID = CHUNK + 8
WIDTH = BLKC * BLOCK
HEIGHT = SPLIT * BLOCK
LEFT = BLOCK // 2
STEPS = 2 * REACH + 1
COUNT = V * BLKC
DEPTH = NBASIS * ROWS_IN
FRESH = {1: (32, 48), 2: (80, 32), 0: (0, 32), 3: (112, 32)}
SINE = [(-1) ** k * math.pi ** (2 * k + 1) / math.factorial(2 * k + 1) for k in range(7)]


def sin_pi(values):
    whole = jnp.floor(values + 0.5)
    rest = values - whole
    odd = whole - 2.0 * jnp.floor(whole * 0.5)
    square = rest * rest
    total = jnp.full(values.shape, SINE[-1], jnp.float32)
    for factor in SINE[-2::-1]:
        total = total * square + factor
    return total * rest * (1.0 - 2.0 * odd)


def lanczos(offset):
    near = jnp.abs(offset) < 1e-4
    safe = jnp.where(near, 1.0, offset)
    value = sin_pi(safe) * sin_pi(safe / 3.0) * (3.0 / math.pi**2) / (safe * safe)
    value = jnp.where(near, 1.0, value)
    return jnp.where(jnp.abs(offset) < 3.0, value, 0.0)


def outward(count):
    far = sorted(range(1, count), key=lambda step: abs(step - count // 2))
    half = len(far) // 2
    near = far[half:][::-1]
    mixed = [step for pair in zip(far[:half], near) for step in pair]
    return mixed + near[half:]


def split(values):
    high = values.astype(jnp.bfloat16)
    return high, (values - high.astype(jnp.float32)).astype(jnp.bfloat16)


def dot(left, right):
    return jnp.dot(left, right, preferred_element_type=jnp.float32)


def band_kernel(
    devices,
    capacity,
    taps_ref,
    coef_ref,
    affine_ref,
    patch_ref,
    slot_ref,
    owner_ref,
    weight_ref,
    image_ref,
    table_ref,
    got_ref,
    ext,
    col_kernel,
    row_kernel,
    lhs,
    terms_high,
    terms_low,
    row_weight,
    col_weight,
    mid,
    stage,
    outbox,
    notes,
    plan,
    sent,
    received,
    own,
    rims,
):
    band = lax.axis_index("ccd")
    barrier = pltpu.get_barrier_semaphore()
    chunks = len(ORDER)
    for step in range(1, devices):
        pl.semaphore_signal(
            barrier,
            inc=1,
            device_id={"ccd": lax.rem(band + step, devices)},
            device_id_type=pl.DeviceIdType.MESH,
        )
    load = pltpu.make_async_copy(image_ref, ext.at[:, pl.ds(RIM, BLOCK)], own.at[chunks + 1])
    load.start()

    shifted = band + SPLIT // 2
    ccd = shifted // SPLIT
    top_row = shifted % SPLIT * BLOCK
    region_shift = band * BLOCK - top_row
    region_low = jnp.maximum(0, -region_shift)
    region_high = jnp.minimum(HEIGHT, devices * BLOCK - region_shift)

    def inside(first, count):
        rows = first + lax.broadcasted_iota(jnp.int32, (count, 1), 0)
        return (rows >= region_low) & (rows < region_high)

    owners = [owner_ref[patch_ref[block]] for block in range(COUNT)]
    lane_row = lax.broadcasted_iota(jnp.int32, (1, BLOCK), 1)
    weight_lane = lax.broadcasted_iota(jnp.int32, weight_ref.shape, 1)
    weights = jnp.sum(
        jnp.where(weight_lane == ccd, weight_ref[...].astype(jnp.float32), 0.0), axis=1, keepdims=True
    )

    def plan_one(device, carry):
        first, last = jnp.int32(COUNT), jnp.int32(-1)
        for block in range(COUNT):
            mine = owners[block] == device
            first = jnp.where(mine & (first == COUNT), block, first)
            last = jnp.where(mine, block, last)
        some = last >= 0
        first = jnp.where(some, first, 0)
        two = some & (last != first)
        last = jnp.where(some, last, 0)
        plan[device * capacity] = first
        plan[device * capacity + 1] = last
        for slot in range(2, capacity):
            plan[device * capacity + slot] = 0
        note = jnp.where(lane_row == 0, slot_ref[0, first], jnp.where(lane_row == 1, slot_ref[0, last], 0))
        note = note.astype(jnp.float32)
        for visit in range(V):
            here = jnp.broadcast_to(weights[visit : visit + 1], (1, BLOCK))
            pick_first = (lane_row == 2) & (some & (first // BLKC == visit))
            pick_last = (lane_row == 3) & (two & (last // BLKC == visit))
            note = jnp.where(pick_first | pick_last, here, note)
        notes[device] = note
        return carry

    lax.fori_loop(0, devices, plan_one, 0)

    low_row, high_row = LEFT - HALF - LEFT % 8 - 3, 200
    low_row = low_row // 16 * 16
    high_row = -(-(LEFT + HALF + BLOCK) // 16) * 16
    spread = high_row - low_row
    distance = (
        low_row
        + lax.broadcasted_iota(jnp.int32, (spread, BLOCK), 0)
        - lax.broadcasted_iota(jnp.int32, (spread, BLOCK), 1)
        - (LEFT - HALF)
    )
    col_kernel[...] = jnp.zeros_like(col_kernel)

    def col_one(basis, carry):
        total = jnp.zeros((spread, BLOCK), jnp.float32)
        for tap in range(TAPS):
            total = jnp.where(distance == tap, taps_ref[basis, 1, tap], total)
        high, low = split(total)
        cols = pl.ds(pl.multiple_of(basis * BLOCK, BLOCK), BLOCK)
        col_kernel[pl.ds(low_row, spread), cols] = high
        col_kernel[pl.ds(2 * BLOCK + low_row, spread), cols] = high
        col_kernel[pl.ds(4 * BLOCK + low_row, spread), cols] = low
        return carry

    lax.fori_loop(0, NBASIS, col_one, 0)

    wide_lane = lax.broadcasted_iota(jnp.int32, (1, DEPTH), 1)
    starts = [wide_lane >= basis * ROWS_IN for basis in range(NBASIS)]

    def by_basis(value):
        total = jnp.full((1, DEPTH), value(0), jnp.float32)
        for basis in range(1, NBASIS):
            total = jnp.where(starts[basis], value(basis), total)
        return total

    start = jnp.zeros((1, DEPTH), jnp.int32)
    for basis in range(1, NBASIS):
        start = jnp.where(starts[basis], basis * ROWS_IN, start)
    gap = (wide_lane - start) - lax.broadcasted_iota(jnp.int32, (ROWS_MID, DEPTH), 0)
    total = jnp.zeros(gap.shape, jnp.float32)
    for tap in range(TAPS):
        total = jnp.where(gap == tap, by_basis(lambda basis: taps_ref[basis, 0, tap]), total)
    row_kernel[...] = total

    lane = lax.broadcasted_iota(jnp.int32, (1, BLOCK), 1)
    base, slope = jnp.zeros((1, BLOCK), jnp.float32), jnp.zeros((1, BLOCK), jnp.float32)
    for visit in range(V):
        base = jnp.where(lane // 8 == visit, affine_ref[visit, 0, 0, ccd], base)
        slope = jnp.where(lane // 8 == visit, affine_ref[visit, 0, 1, ccd], slope)
    own_rows = (top_row + lax.broadcasted_iota(jnp.int32, (BLOCK, BLOCK), 0)).astype(jnp.float32)
    row_shift = base + slope * ((own_rows - (HEIGHT - 1) / 2.0) / HEIGHT)
    row_step = (lane % 8 - REACH).astype(jnp.float32)
    all_rows = lanczos(row_shift - row_step)
    column = lax.broadcasted_iota(jnp.int32, (1, WIDTH), 1).astype(jnp.float32)
    col_pos = (2.0 * column + 1.0) / WIDTH - 1.0
    col_step = lax.broadcasted_iota(jnp.int32, (8, WIDTH), 0) - REACH
    reached = lax.broadcasted_iota(jnp.int32, (8, WIDTH), 1) + col_step
    for visit in range(V):
        row_weight[visit] = all_rows if visit == 0 else pltpu.roll(all_rows, BLOCK - 8 * visit, 1)
        col_shift = affine_ref[visit, 1, 0, ccd] + affine_ref[visit, 1, 1, ccd] * (
            (column - (WIDTH - 1) / 2.0) / WIDTH
        )
        col_weight[visit] = jnp.where(
            (reached >= 0) & (reached < WIDTH), lanczos(col_shift - col_step.astype(jnp.float32)), 0.0
        )

    def remote(source, target, kind, step):
        return pltpu.make_async_remote_copy(
            src_ref=source,
            dst_ref=target,
            send_sem=sent.at[kind, step],
            recv_sem=received.at[kind, step],
            device_id={"ccd": lax.rem(band + step, devices)},
            device_id_type=pl.DeviceIdType.MESH,
        )

    has_next, has_last = band < devices - 1, band > 0

    def to_next():
        return pltpu.make_async_remote_copy(
            src_ref=image_ref.at[:, pl.ds(BLOCK - RIM, RIM)],
            dst_ref=ext.at[:, pl.ds(0, RIM)],
            send_sem=rims.at[0],
            recv_sem=rims.at[1],
            device_id={"ccd": lax.rem(band + 1, devices)},
            device_id_type=pl.DeviceIdType.MESH,
        )

    def to_last():
        return pltpu.make_async_remote_copy(
            src_ref=image_ref.at[:, pl.ds(0, RIM)],
            dst_ref=ext.at[:, pl.ds(RIM + BLOCK, RIM)],
            send_sem=rims.at[2],
            recv_sem=rims.at[3],
            device_id={"ccd": lax.rem(band + devices - 1, devices)},
            device_id_type=pl.DeviceIdType.MESH,
        )

    load.wait()
    waits = []
    for turn, chunk in enumerate(ORDER):
        if chunk == 0:
            @pl.when(has_next)
            def _():
                to_next().wait_send()
                to_last().wait_recv()

            @pl.when(has_last)
            def _():
                to_last().wait_send()
                to_next().wait_recv()

        fresh, fresh_rows = FRESH[chunk]
        for visit in range(V):
            raw = ext[visit, fresh : fresh + fresh_rows]
            raw = jnp.where(inside(top_row + fresh - RIM, fresh_rows), raw, 0.0)
            side = jnp.zeros((fresh_rows, LEFT), jnp.bfloat16)
            high, low = (jnp.concatenate([side, part, side], axis=1) for part in split(raw))
            for block in range(BLKC):
                rows = pl.ds((block * V + visit) * fresh_rows, fresh_rows)
                window = slice(block * BLOCK, (block + 2) * BLOCK)
                lhs[rows, 0 : 2 * BLOCK] = high[:, window]
                lhs[rows, 2 * BLOCK : 4 * BLOCK] = low[:, window]
        done = COUNT * fresh_rows
        for basis in range(NBASIS):
            cols = pl.ds(basis * BLOCK, BLOCK)
            left = jnp.concatenate([lhs[0:done, :], lhs[0:done, 0 : 2 * BLOCK]], axis=1)
            high, low = split(dot(left, col_kernel[:, cols]))
            for block in range(BLKC):
                for visit in range(V):
                    rows = slice((block * V + visit) * fresh_rows, (block * V + visit + 1) * fresh_rows)
                    into = pl.ds(fresh, fresh_rows), pl.ds(block * BLOCK, BLOCK)
                    terms_high[visit, basis, into[0], into[1]] = high[rows]
                    terms_low[visit, basis, into[0], into[1]] = low[rows]

        first = top_row + chunk * CHUNK

        def one_visit(visit, carry, chunk=chunk, first=first):
            position = (first - REACH + lax.broadcasted_iota(jnp.int32, (ROWS_MID, 1), 0)).astype(
                jnp.float32
            )
            row_pos = (2.0 * position + 1.0) / HEIGHT - 1.0
            kernel = row_kernel[...]
            constant, by_row, by_column = (
                by_basis(lambda basis: coef_ref[ccd, part, visit, basis]) for part in range(3)
            )
            level = kernel * (constant + by_row * row_pos)
            high, low = split(jnp.concatenate([level, kernel * by_column], axis=0))
            rows = pl.ds(chunk * CHUNK, ROWS_IN)
            upper = dot(
                jnp.concatenate([high, low], axis=0), terms_high[visit, :, rows, :].reshape(DEPTH, WIDTH)
            )
            lower = dot(high, terms_low[visit, :, rows, :].reshape(DEPTH, WIDTH))
            both = upper[: 2 * ROWS_MID] + upper[2 * ROWS_MID :] + lower
            matched = both[:ROWS_MID] + both[ROWS_MID:] * col_pos
            mid[...] = jnp.where(inside(first - REACH, ROWS_MID), matched, 0.0)

            weight = row_weight[visit, pl.ds(chunk * CHUNK, CHUNK)]
            warped = jnp.zeros((CHUNK, WIDTH), jnp.float32)
            for step in range(STEPS):
                warped = warped + weight[:, step : step + 1] * mid[step : step + CHUNK, :]
            weight = col_weight[visit]
            total = jnp.zeros((CHUNK, WIDTH), jnp.float32)
            for step in range(STEPS):
                offset = step - REACH
                moved = warped if offset == 0 else pltpu.roll(warped, (-offset) % WIDTH, 1)
                total = total + weight[step : step + 1, :] * moved
            rounded = total.astype(jnp.bfloat16)
            for block in range(BLKC):
                stage[turn % 2, visit * BLKC + block] = rounded[:, block * BLOCK : (block + 1) * BLOCK]
            return carry

        lax.fori_loop(0, V, one_visit, 0)
        rows = pl.ds(chunk * CHUNK, CHUNK)
        for device in range(devices):
            for slot in range(capacity):
                outbox[device, slot, rows] = stage[turn % 2, plan[device * capacity + slot]]
        if turn == 0:
            pl.semaphore_wait(barrier, devices - 1)

            @pl.when(has_next)
            def _():
                to_next().start()

            @pl.when(has_last)
            def _():
                to_last().start()

        batch = []
        for step in outward(devices):
            target = lax.rem(band + step, devices)
            batch.append(
                remote(outbox.at[target, :, rows], got_ref.at[band, :, rows], chunk, step)
            )
        batch.append(
            pltpu.make_async_copy(outbox.at[band, :, rows], got_ref.at[band, :, rows], own.at[chunk])
        )
        if turn == 0:
            for step in outward(devices):
                batch.append(
                    remote(notes.at[lax.rem(band + step, devices)], table_ref.at[band], chunks, step)
                )
            batch.append(pltpu.make_async_copy(notes.at[band], table_ref.at[band], own.at[chunks]))
        for copy in batch:
            copy.start()
        waits += batch
    for copy in waits:
        copy.wait()


def gather_kernel(devices, capacity, table_ref, got_ref, out_ref, blocks, total, weights, sems):
    loads = [
        pltpu.make_async_copy(got_ref.at[source], blocks.at[source], sems.at[source])
        for source in range(devices)
    ]
    for load in loads:
        load.start()
    total[...] = jnp.zeros_like(total)
    for cell in range(CELLS):
        weights[cell] = 0.0
    for load in loads:
        load.wait()

    def add(source, carry):
        for slot in range(2):
            weight = table_ref[source, 0, 2 + slot]

            @pl.when(weight > 0.0)
            def _():
                cell = table_ref[source, 0, slot].astype(jnp.int32)
                weights[cell] = weights[cell] + weight
                total[cell] = total[cell] + weight * blocks[source, slot].astype(jnp.float32)

        return carry

    lax.fori_loop(0, devices, add, 0)
    for cell in range(CELLS):
        row, col = cell // PSIDE * BLOCK, cell % PSIDE * BLOCK
        scale = 1.0 / jnp.full((1, BLOCK), jnp.maximum(weights[cell], 1.0), jnp.float32)
        out_ref[0, row : row + BLOCK, col : col + BLOCK] = total[cell] * scale


def shards(
    images, basis_taps, psf_coef, affine, visit_weight, block_patch, block_slot, patch_owner
):
    devices = lax.axis_size("ccd")
    capacity = max(2, (2 * COUNT + devices - 1) // devices)
    anywhere = pl.BlockSpec(memory_space=pl.ANY)
    scalars = pl.BlockSpec(memory_space=pltpu.SMEM)
    vector = pl.BlockSpec(memory_space=pltpu.VMEM)
    chunks = len(ORDER)
    half = jnp.bfloat16
    table, got = pl.pallas_call(
        functools.partial(band_kernel, devices, capacity),
        out_shape=(
            jax.ShapeDtypeStruct((devices, 1, BLOCK), jnp.float32),
            jax.ShapeDtypeStruct((devices, capacity, BLOCK, BLOCK), half),
        ),
        in_specs=[scalars] * 6 + [vector, anywhere],
        out_specs=(vector, anywhere),
        scratch_shapes=[
            pltpu.VMEM((V, EXT, WIDTH), jnp.float32),
            pltpu.VMEM((6 * BLOCK, NBASIS * BLOCK), half),
            pltpu.VMEM((ROWS_MID, DEPTH), jnp.float32),
            pltpu.VMEM((COUNT * ROWS_IN, 4 * BLOCK), half),
            pltpu.VMEM((V, NBASIS, EXT, WIDTH), half),
            pltpu.VMEM((V, NBASIS, EXT, WIDTH), half),
            pltpu.VMEM((V, BLOCK, BLOCK), jnp.float32),
            pltpu.VMEM((V, 8, WIDTH), jnp.float32),
            pltpu.VMEM((ROWS_MID, WIDTH), jnp.float32),
            pltpu.VMEM((2, COUNT, CHUNK, BLOCK), half),
            pltpu.VMEM((devices, capacity, BLOCK, BLOCK), half),
            pltpu.VMEM((devices, 1, BLOCK), jnp.float32),
            pltpu.SMEM((devices * capacity,), jnp.int32),
            pltpu.SemaphoreType.DMA((chunks + 1, devices)),
            pltpu.SemaphoreType.DMA((chunks + 1, devices)),
            pltpu.SemaphoreType.DMA((chunks + 2,)),
            pltpu.SemaphoreType.DMA((4,)),
        ],
        compiler_params=pltpu.CompilerParams(collective_id=1, has_side_effects=True),
    )(
        basis_taps.transpose(1, 0, 2),
        psf_coef.transpose(1, 3, 0, 2),
        affine.transpose(0, 2, 3, 1),
        block_patch.reshape(-1),
        block_slot,
        patch_owner,
        visit_weight,
        images,
    )
    size = PSIDE * BLOCK
    return pl.pallas_call(
        functools.partial(gather_kernel, devices, capacity),
        out_shape=jax.ShapeDtypeStruct((1, size, size), jnp.float32),
        in_specs=[scalars, anywhere],
        out_specs=vector,
        scratch_shapes=[
            pltpu.VMEM((devices, capacity, BLOCK, BLOCK), half),
            pltpu.VMEM((CELLS, BLOCK, BLOCK), jnp.float32),
            pltpu.SMEM((CELLS,), jnp.float32),
            pltpu.SemaphoreType.DMA((devices,)),
        ],
    )(table, got)


def solution(mesh):
    placed = (
        P(None, ("group", "ccd"), None),
        P(),
        P(None, "group", None, None),
        P(None, "group", None, None),
        P(None, "group"),
        P(("group", "ccd"), None, None),
        P(("group", "ccd"), None),
        P("group"),
    )
    return jax.shard_map(
        shards,
        mesh=mesh,
        in_specs=placed,
        out_specs=P(("group", "ccd"), None, None),
        check_vma=False,
    )
```

time: 55.7 us -> 43.1 us (0.77)
  Pallas kernels: 51.6 us -> 42.7 us
  local copies, waits for them, and re-layouts: 2.47 us -> 0 us
  other arithmetic: 1.26 us -> 0 us
    pallas_call x2 -> x0, Pallas kernels: 5.67 us -> none  [the longest x1 4.23 us: shards(): pl.pallas_call(functools.partial(rim_kernel, devices), out_shape=(rim_sha...]
    pallas_call x1, Pallas kernels: 40.9 us -> 38.8 us  [shards(): pl.pallas_call(functools.partial(band_kernel, devices, capacity), out_sha...]
    unnamed x9 -> x0, local copies, waits for them, and re-layouts: 1.68 us -> none
    convert_element_type x1 -> x0, other arithmetic: 1.26 us -> none  [shards(): visit_weight.astype(jnp.float32)]
    pallas_call x1, Pallas kernels: 5.07 us -> 3.9 us  [shards(): pl.pallas_call(functools.partial(gather_kernel, devices, capacity), out_s...]
    reshape x1 -> x0, local copies, waits for them, and re-layouts: 0.79 us -> none  [shards(): psf_coef.reshape(-1)]
where the time goes in v1:
time: 43.1 us; the launch traced here: 42.7 us
  Pallas kernels  42.7 us (99%)
    pallas_call x1, Pallas kernels, shards(): pl.pallas_call(functools.partial(band_kernel, devices, capacity), out_sha...  38.8 us
    pallas_call x1, Pallas kernels, shards(): pl.pallas_call(functools.partial(gather_kernel, devices, capacity), out_s...  3.9 us

profile of v1, /device:TPU:0, one launch (start us, length us, event | category | flops | bytes accessed | tf_op | source)
XLA Modules:
  0.0 42.7 jit_solution(17430359795684585474)
XLA Ops:
  0.0 38.8 %shard_map.82 = (f32[16,1,128]{2,1,0:T(1,128)}, bf16[16,2,128,128]{3,2,1,0:T(8,128)(2,1)}) custom-call(f32[9,2,11]{2,1,0:T(2,128)} %bitcast.5, f32[5,3,4,9]{3,2,1,0:T(4,128)} %bitcast.4, f32[4,2,2,5]{3,2,1,0:T(2,128)} %bitcast.6, s32[16]{0:T(128)} %bitcast.7, s32[1,16]{1,0:T(1,128)} %slot_ref.1, s32[16]{0:T(128)} %owner_ref.1, bf16[4,5]{1,0:T(4,128)(2,1)} %weight_ref.1, ...), custom_call_target="tpu_custom_call" | custom-call | tf_op jit(solution)/shard_map/pallas_call | solution.py:412
  38.8 3.9 %shard_map.83 = f32[1,512,512]{2,1,0:T(8,128)} custom-call(f32[16,1,128]{2,1,0:T(1,128)} %get-tuple-element.7.table_ref, bf16[16,2,128,128]{3,2,1,0:T(8,128)(2,1)} %get-tuple-element.8.got_ref), custom_call_target="tpu_custom_call" | custom-call | tf_op jit(solution)/shard_map/pallas_call | solution.py:451

commit v2 on v1

v2 whole, which is shorter than its diff:
```python
import functools
import math

import jax
import jax.numpy as jnp
from jax import lax
from jax.experimental import pallas as pl
from jax.experimental.pallas import tpu as pltpu
from jax.sharding import PartitionSpec as P

V = 4
BLOCK = 128
BLKC = 4
SPLIT = 4
TAPS = 11
NBASIS = 9
PSIDE = 4
CELLS = PSIDE * PSIDE
HALF = TAPS // 2
REACH = 3
RIM = HALF + REACH
CHUNK = 32
CAP = 2
GROUP = 16
EXT = BLOCK + 2 * RIM
ROWS_IN = CHUNK + 2 * RIM
ROWS_MID = CHUNK + 8
WIDTH = BLKC * BLOCK
HEIGHT = SPLIT * BLOCK
LEFT = 16
WINDOW = BLOCK + 2 * LEFT
STEPS = 2 * REACH + 1
COUNT = V * BLKC
DEPTH = NBASIS * ROWS_IN
ORDER = (1, 2, 0, 3)
FRESH = ((32, 48), (80, 32), (0, 32), (112, 32))
SENDS = ((0,), (1,), (2, 3))
SINE = [(-1) ** k * math.pi ** (2 * k + 1) / math.factorial(2 * k + 1) for k in range(7)]


def sin_pi(values):
    whole = jnp.floor(values + 0.5)
    rest = values - whole
    odd = whole - 2.0 * jnp.floor(whole * 0.5)
    square = rest * rest
    total = jnp.full(values.shape, SINE[-1], jnp.float32)
    for factor in SINE[-2::-1]:
        total = total * square + factor
    return total * rest * (1.0 - 2.0 * odd)


def finish(product, offset):
    near = jnp.abs(offset) < 1e-4
    square = jnp.where(near, 1.0, offset * offset)
    value = jnp.where(near, 1.0, product * (3.0 / math.pi**2) / square)
    return jnp.where(jnp.abs(offset) < 3.0, value, 0.0)


def lanczos(offset):
    return finish(sin_pi(offset) * sin_pi(offset / 3.0), offset)


def outward(count):
    far = sorted(range(1, count), key=lambda step: abs(step - count // 2))
    half = len(far) // 2
    near = far[half:][::-1]
    mixed = [step for pair in zip(far[:half], near) for step in pair]
    return mixed + near[half:]


def split(values):
    high = values.astype(jnp.bfloat16)
    return high, (values - high.astype(jnp.float32)).astype(jnp.bfloat16)


def dot(left, right):
    return jnp.dot(left, right, preferred_element_type=jnp.float32)


def band_kernel(
    devices,
    taps_ref,
    coef_ref,
    affine_ref,
    patch_ref,
    slot_ref,
    owner_ref,
    weight_ref,
    image_ref,
    out_ref,
    ext,
    col_kernel,
    lhs,
    terms_high,
    terms_low,
    mid,
    stage,
    outbox,
    inbox,
    notes,
    table,
    picks,
    plan,
    sent,
    received,
    own,
    rims,
):
    band = lax.axis_index("ccd")
    barrier = pltpu.get_barrier_semaphore()
    sends = len(SENDS)
    for step in range(1, devices):
        pl.semaphore_signal(
            barrier,
            inc=1,
            device_id={"ccd": lax.rem(band + step, devices)},
            device_id_type=pl.DeviceIdType.MESH,
        )
    load = pltpu.make_async_copy(image_ref, ext.at[:, pl.ds(RIM, BLOCK)], own.at[sends + 1])
    load.start()

    shifted = band + SPLIT // 2
    ccd = shifted // SPLIT
    top_row = shifted % SPLIT * BLOCK
    region_shift = band * BLOCK - top_row
    region_low = jnp.maximum(0, -region_shift)
    region_high = jnp.minimum(HEIGHT, devices * BLOCK - region_shift)
    lane = lax.broadcasted_iota(jnp.int32, (1, BLOCK), 1)

    def inside(first, count):
        rows = first + lax.broadcasted_iota(jnp.int32, (count, 1), 0)
        return (rows >= region_low) & (rows < region_high)

    weight_lane = lax.broadcasted_iota(jnp.int32, weight_ref.shape, 1)
    weights = jnp.sum(
        jnp.where(weight_lane == ccd, weight_ref[...].astype(jnp.float32), 0.0), axis=1, keepdims=True
    )
    owners = jnp.full((1, BLOCK), -1, jnp.int32)
    cells = jnp.zeros((1, BLOCK), jnp.float32)
    block_weight = jnp.zeros((1, BLOCK), jnp.float32)
    for block in range(COUNT):
        owners = jnp.where(lane == block, owner_ref[patch_ref[block]], owners)
        cells = jnp.where(lane == block, slot_ref[0, block].astype(jnp.float32), cells)
    for visit in range(V):
        here = jnp.broadcast_to(weights[visit : visit + 1], (1, BLOCK))
        block_weight = jnp.where(lane // BLKC == visit, here, block_weight)
    lanes = lax.broadcasted_iota(jnp.int32, (devices, BLOCK), 1)
    match = owners == lax.broadcasted_iota(jnp.int32, (devices, BLOCK), 0)
    first = jnp.min(jnp.where(match, lanes, BLOCK), axis=1, keepdims=True)
    last = jnp.max(jnp.where(match, lanes, -1), axis=1, keepdims=True)
    is_first, is_last = lanes == first, lanes == last

    def at(chosen, values):
        return jnp.sum(jnp.where(chosen, values, 0.0), axis=1, keepdims=True)

    note = jnp.where(
        lanes < 2 * GROUP,
        jnp.where(lanes < GROUP, at(is_first, cells), at(is_last, cells)),
        jnp.where(
            lanes < 3 * GROUP, at(is_first, block_weight), at(is_last & (last > first), block_weight)
        ),
    )
    picks[...] = jnp.where(lanes == 0, jnp.where(last < 0, 0, first), jnp.maximum(last, 0))
    to_plan = pltpu.make_async_copy(picks, plan, own.at[sends + 2])
    to_plan.start()
    for device in range(devices):
        notes[device] = note[device : device + 1]

    sub = lax.broadcasted_iota(jnp.int32, (8, BLOCK), 0)
    across = lax.broadcasted_iota(jnp.int32, (8, BLOCK), 1)
    edge = LEFT - HALF
    for basis in range(NBASIS):
        taps = jnp.zeros((8, BLOCK), jnp.float32)
        for tap in range(TAPS):
            taps = jnp.where(across == BLOCK - edge - tap, taps_ref[basis, 1, tap], taps)
        taps = pltpu.roll(taps, 0, 1, stride=1, stride_axis=0)
        high = taps.astype(jnp.bfloat16).astype(jnp.float32)
        low = taps - high
        cols = slice(basis * BLOCK, (basis + 1) * BLOCK)
        for part, offsets in ((high, (0, WINDOW)), (low, (2 * WINDOW,))):
            rows = []
            for group in range(WINDOW // 8):
                turned = pltpu.roll(part, group * 8 % BLOCK, 1) if group * 8 % BLOCK else part
                tap = group * 8 + sub - edge - across
                rows.append(jnp.where((tap >= 0) & (tap < TAPS), turned, 0.0))
            matrix = jnp.concatenate(rows, axis=0).astype(jnp.bfloat16)
            for offset in offsets:
                col_kernel[offset : offset + WINDOW, cols] = matrix

    wide_lane = lax.broadcasted_iota(jnp.int32, (1, DEPTH), 1)
    starts = [wide_lane >= basis * ROWS_IN for basis in range(NBASIS)]

    def by_basis(value):
        total = jnp.full((1, DEPTH), value(0), jnp.float32)
        for basis in range(1, NBASIS):
            total = jnp.where(starts[basis], value(basis), total)
        return total

    start = jnp.zeros((1, DEPTH), jnp.int32)
    for basis in range(1, NBASIS):
        start = jnp.where(starts[basis], basis * ROWS_IN, start)
    gap = (wide_lane - start) - lax.broadcasted_iota(jnp.int32, (ROWS_MID, DEPTH), 0)
    row_kernel = jnp.zeros(gap.shape, jnp.float32)
    for tap in range(TAPS):
        row_kernel = jnp.where(gap == tap, by_basis(lambda basis: taps_ref[basis, 0, tap]), row_kernel)

    column = lax.broadcasted_iota(jnp.int32, (1, WIDTH), 1).astype(jnp.float32)
    col_pos = (2.0 * column + 1.0) / WIDTH - 1.0
    line = lax.broadcasted_iota(jnp.int32, (8, 1), 0)
    base, slope = jnp.zeros((8, 1), jnp.float32), jnp.zeros((8, 1), jnp.float32)
    for visit in range(V):
        base = jnp.where(line == visit, affine_ref[visit, 1, 0, ccd], base)
        slope = jnp.where(line == visit, affine_ref[visit, 1, 1, ccd], slope)
    col_shift = base + slope * ((column - (WIDTH - 1) / 2.0) / WIDTH)
    sine = sin_pi(col_shift)
    third_sine, third_cosine = sin_pi(col_shift / 3.0), sin_pi(col_shift / 3.0 + 0.5)
    turn_cos, turn_sin = jnp.zeros((8, 1), jnp.float32), jnp.zeros((8, 1), jnp.float32)
    for step in range(STEPS):
        k = step - REACH
        turn_cos = jnp.where(line == step, (-1) ** k * math.cos(math.pi * k / 3), turn_cos)
        turn_sin = jnp.where(line == step, (-1) ** k * math.sin(math.pi * k / 3), turn_sin)
    col_step = lax.broadcasted_iota(jnp.int32, (8, WIDTH), 0) - REACH
    reached = lax.broadcasted_iota(jnp.int32, (8, WIDTH), 1) + col_step
    reached = (reached >= 0) & (reached < WIDTH)
    col_weight = []
    for visit in range(V):
        row = slice(visit, visit + 1)
        product = sine[row] * (third_sine[row] * turn_cos - third_cosine[row] * turn_sin)
        weight = finish(product, col_shift[row] - col_step.astype(jnp.float32))
        col_weight.append(jnp.where(reached, weight, 0.0))

    row_base, row_slope = jnp.zeros((1, BLOCK), jnp.float32), jnp.zeros((1, BLOCK), jnp.float32)
    for visit in range(V):
        row_base = jnp.where(lane // 8 == visit, affine_ref[visit, 0, 0, ccd], row_base)
        row_slope = jnp.where(lane // 8 == visit, affine_ref[visit, 0, 1, ccd], row_slope)
    row_step = (lane % 8 - REACH).astype(jnp.float32)

    def remote(source, target, kind, step):
        return pltpu.make_async_remote_copy(
            src_ref=source,
            dst_ref=target,
            send_sem=sent.at[kind, step],
            recv_sem=received.at[kind, step],
            device_id={"ccd": lax.rem(band + step, devices)},
            device_id_type=pl.DeviceIdType.MESH,
        )

    has_next, has_last = band < devices - 1, band > 0

    def to_next():
        return pltpu.make_async_remote_copy(
            src_ref=image_ref.at[:, pl.ds(BLOCK - RIM, RIM)],
            dst_ref=ext.at[:, pl.ds(0, RIM)],
            send_sem=rims.at[0],
            recv_sem=rims.at[1],
            device_id={"ccd": lax.rem(band + 1, devices)},
            device_id_type=pl.DeviceIdType.MESH,
        )

    def to_last():
        return pltpu.make_async_remote_copy(
            src_ref=image_ref.at[:, pl.ds(0, RIM)],
            dst_ref=ext.at[:, pl.ds(RIM + BLOCK, RIM)],
            send_sem=rims.at[2],
            recv_sem=rims.at[3],
            device_id={"ccd": lax.rem(band + devices - 1, devices)},
            device_id_type=pl.DeviceIdType.MESH,
        )

    load.wait()
    batches = []
    for turn, chunk in enumerate(ORDER):
        if chunk == 0:
            @pl.when(has_next)
            def _():
                to_next().wait_send()
                to_last().wait_recv()

            @pl.when(has_last)
            def _():
                to_last().wait_send()
                to_next().wait_recv()

        fresh, count = FRESH[turn]
        for visit in range(V):
            raw = ext[visit, fresh : fresh + count]
            raw = jnp.where(inside(top_row + fresh - RIM, count), raw, 0.0)
            side = jnp.zeros((count, LEFT), jnp.bfloat16)
            high, low = (jnp.concatenate([side, part, side], axis=1) for part in split(raw))
            for block in range(BLKC):
                rows = slice((block * V + visit) * count, (block * V + visit + 1) * count)
                window = slice(block * BLOCK, block * BLOCK + WINDOW)
                lhs[rows, 0:WINDOW] = high[:, window]
                lhs[rows, WINDOW : 2 * WINDOW] = low[:, window]
                lhs[rows, 2 * WINDOW : 3 * WINDOW] = high[:, window]
        for pair in range(0, NBASIS, 2):
            bases = range(pair, min(pair + 2, NBASIS))
            cols = slice(pair * BLOCK, (bases[-1] + 1) * BLOCK)
            high, low = split(dot(lhs[0 : COUNT * count, :], col_kernel[:, cols]))
            for block in range(BLKC):
                for visit in range(V):
                    rows = slice((block * V + visit) * count, (block * V + visit + 1) * count)
                    for basis in bases:
                        part = slice((basis - pair) * BLOCK, (basis - pair + 1) * BLOCK)
                        into = slice(fresh, fresh + count), slice(block * BLOCK, (block + 1) * BLOCK)
                        terms_high[visit, basis, into[0], into[1]] = high[rows, part]
                        terms_low[visit, basis, into[0], into[1]] = low[rows, part]

        top = top_row + chunk * CHUNK
        own_rows = (top + lax.broadcasted_iota(jnp.int32, (CHUNK, 1), 0)).astype(jnp.float32)
        row_shift = row_base + row_slope * ((own_rows - (HEIGHT - 1) / 2.0) / HEIGHT)
        row_weight = lanczos(row_shift - row_step)
        position = (top - REACH + lax.broadcasted_iota(jnp.int32, (ROWS_MID, 1), 0)).astype(jnp.float32)
        row_pos = (2.0 * position + 1.0) / HEIGHT - 1.0
        keep = inside(top - REACH, ROWS_MID)
        for visit in range(V):
            constant, by_row, by_column = (
                by_basis(lambda basis: coef_ref[ccd, part, visit, basis]) for part in range(3)
            )
            level = row_kernel * (constant + by_row * row_pos)
            high, low = split(jnp.concatenate([level, row_kernel * by_column], axis=0))
            rows = slice(chunk * CHUNK, chunk * CHUNK + ROWS_IN)
            upper = dot(
                jnp.concatenate([high, low], axis=0), terms_high[visit, :, rows, :].reshape(DEPTH, WIDTH)
            )
            lower = dot(high, terms_low[visit, :, rows, :].reshape(DEPTH, WIDTH))
            both = upper[: 2 * ROWS_MID] + upper[2 * ROWS_MID :] + lower
            matched = both[:ROWS_MID] + both[ROWS_MID:] * col_pos
            mid[visit] = jnp.where(keep, matched, 0.0)

            warped = jnp.zeros((CHUNK, WIDTH), jnp.float32)
            for step in range(STEPS):
                column_of = visit * 8 + step
                warped = warped + row_weight[:, column_of : column_of + 1] * mid[visit, step : step + CHUNK, :]
            total = jnp.zeros((CHUNK, WIDTH), jnp.float32)
            for step in range(STEPS):
                offset = step - REACH
                moved = warped if offset == 0 else pltpu.roll(warped, (-offset) % WIDTH, 1)
                total = total + col_weight[visit][step : step + 1, :] * moved
            rounded = total.astype(jnp.bfloat16)
            for block in range(BLKC):
                stage[turn, visit * BLKC + block] = rounded[:, block * BLOCK : (block + 1) * BLOCK]

        if turn == 0:
            to_plan.wait()
        rows = slice(turn * CHUNK, (turn + 1) * CHUNK)
        for device in range(devices):
            for slot in range(CAP):
                pick = jnp.minimum(jnp.maximum(plan[device, slot], 0), COUNT - 1)
                outbox[device, slot, rows] = stage[turn, pick]
        if turn == 0:
            pl.semaphore_wait(barrier, devices - 1)

            @pl.when(has_next)
            def _():
                to_next().start()

            @pl.when(has_last)
            def _():
                to_last().start()

        for send, turns in enumerate(SENDS):
            if turns[-1] != turn:
                continue
            rows = pl.ds(turns[0] * CHUNK, len(turns) * CHUNK)
            batch = []
            for step in outward(devices):
                target = lax.rem(band + step, devices)
                batch.append(
                    remote(outbox.at[target, :, rows], inbox.at[band, :, rows], send, step)
                )
            batch.append(
                pltpu.make_async_copy(outbox.at[band, :, rows], inbox.at[band, :, rows], own.at[send])
            )
            for copy in batch:
                copy.start()
            batches.append(batch)
        if turn == 0:
            batch = []
            for step in outward(devices):
                batch.append(
                    remote(notes.at[lax.rem(band + step, devices)], table.at[band], sends, step)
                )
            batch.append(pltpu.make_async_copy(notes.at[band], table.at[band], own.at[sends]))
            for copy in batch:
                copy.start()
            note_batch = batch

    for copy in note_batch:
        copy.wait()
    per_tile = BLOCK // (CAP * GROUP)
    cell_tiles, weight_tiles = [], []
    for tile in range(devices // per_tile):
        cell_tile = jnp.zeros((1, BLOCK), jnp.float32)
        weight_tile = jnp.zeros((1, BLOCK), jnp.float32)
        for part in range(per_tile):
            row = table[tile * per_tile + part]
            here = lane // (CAP * GROUP) == part
            cell_tile = jnp.where(here, pltpu.roll(row, part * CAP * GROUP, 1) if part else row, cell_tile)
            shift = (part - 1) * CAP * GROUP % BLOCK
            weight_tile = jnp.where(here, pltpu.roll(row, shift, 1) if shift else row, weight_tile)
        cell_tiles.append(cell_tile)
        weight_tiles.append(weight_tile)
    cell_of = jnp.concatenate(cell_tiles, axis=1)
    weight_of = jnp.concatenate(weight_tiles, axis=1)
    span = devices * CAP * GROUP
    diagonal = lax.broadcasted_iota(jnp.int32, (GROUP, span), 1) % GROUP == lax.broadcasted_iota(
        jnp.int32, (GROUP, span), 0
    )
    mixing = jnp.concatenate(
        [
            jnp.where(diagonal & (cell_of == float(cell)), weight_of, 0.0).astype(jnp.bfloat16)
            for cell in range(CELLS)
        ],
        axis=0,
    )
    sums = dot(mixing, jnp.ones((span, BLOCK), jnp.bfloat16))
    scale = 1.0 / jnp.maximum(sums, 1.0)
    for batch, turns in zip(batches, SENDS):
        for copy in batch:
            copy.wait()
        for turn in turns:
            groups = range(turn * CHUNK, (turn + 1) * CHUNK, GROUP)
            blocks = jnp.concatenate(
                [inbox[:, :, group : group + GROUP, :].reshape(span, BLOCK) for group in groups], axis=1
            )
            result = dot(mixing, blocks)
            for index, group in enumerate(groups):
                part = result[:, index * BLOCK : (index + 1) * BLOCK] * scale
                row = ORDER[turn] * CHUNK + index * GROUP
                for cell in range(CELLS):
                    out_ref[
                        0,
                        cell // PSIDE * BLOCK + row : cell // PSIDE * BLOCK + row + GROUP,
                        cell % PSIDE * BLOCK : (cell % PSIDE + 1) * BLOCK,
                    ] = part[cell * GROUP : (cell + 1) * GROUP]


def shards(
    images, basis_taps, psf_coef, affine, visit_weight, block_patch, block_slot, patch_owner
):
    devices = lax.axis_size("ccd")
    scalars = pl.BlockSpec(memory_space=pltpu.SMEM)
    vector = pl.BlockSpec(memory_space=pltpu.VMEM)
    sends = len(SENDS)
    half = jnp.bfloat16
    size = PSIDE * BLOCK
    return pl.pallas_call(
        functools.partial(band_kernel, devices),
        out_shape=jax.ShapeDtypeStruct((1, size, size), jnp.float32),
        in_specs=[scalars] * 6 + [vector, pl.BlockSpec(memory_space=pl.ANY)],
        out_specs=vector,
        scratch_shapes=[
            pltpu.VMEM((V, EXT, WIDTH), jnp.float32),
            pltpu.VMEM((3 * WINDOW, NBASIS * BLOCK), half),
            pltpu.VMEM((COUNT * ROWS_IN, 3 * WINDOW), half),
            pltpu.VMEM((V, NBASIS, EXT, WIDTH), half),
            pltpu.VMEM((V, NBASIS, EXT, WIDTH), half),
            pltpu.VMEM((V, ROWS_MID, WIDTH), jnp.float32),
            pltpu.VMEM((len(ORDER), COUNT, CHUNK, BLOCK), half),
            pltpu.VMEM((devices, CAP, BLOCK, BLOCK), half),
            pltpu.VMEM((devices, CAP, BLOCK, BLOCK), half),
            pltpu.VMEM((devices, 1, BLOCK), jnp.float32),
            pltpu.VMEM((devices, 1, BLOCK), jnp.float32),
            pltpu.VMEM((devices, BLOCK), jnp.int32),
            pltpu.SMEM((devices, BLOCK), jnp.int32),
            pltpu.SemaphoreType.DMA((sends + 1, devices)),
            pltpu.SemaphoreType.DMA((sends + 1, devices)),
            pltpu.SemaphoreType.DMA((sends + 3,)),
            pltpu.SemaphoreType.DMA((4,)),
        ],
        compiler_params=pltpu.CompilerParams(collective_id=1, has_side_effects=True),
    )(
        basis_taps.transpose(1, 0, 2),
        psf_coef.transpose(1, 3, 0, 2),
        affine.transpose(0, 2, 3, 1),
        block_patch.reshape(-1),
        block_slot,
        patch_owner,
        visit_weight,
        images,
    )


def solution(mesh):
    placed = (
        P(None, ("group", "ccd"), None),
        P(),
        P(None, "group", None, None),
        P(None, "group", None, None),
        P(None, "group"),
        P(("group", "ccd"), None, None),
        P(("group", "ccd"), None),
        P("group"),
    )
    return jax.shard_map(
        shards,
        mesh=mesh,
        in_specs=placed,
        out_specs=P(("group", "ccd"), None, None),
        check_vma=False,
    )
```

time: 43.1 us -> 37.9 us (0.88)
  Pallas kernels: 42.7 us -> 35.3 us
  local copies, waits for them, and re-layouts: 0 us -> 2.26 us
    pallas_call x2 -> x1, Pallas kernels: 42.7 us -> 35.3 us  [shards(): pl.pallas_call(functools.partial(band_kernel, devices), out_shape=jax.Sha...]
    unnamed x0 -> x1, local copies, waits for them, and re-layouts: none -> 2.26 us
where the time goes in v2:
time: 37.9 us; the launch traced here: 37.6 us
  Pallas kernels  35.3 us (93%)
  local copies, waits for them, and re-layouts  2.26 us (6%)
    pallas_call x1, Pallas kernels, shards(): pl.pallas_call(functools.partial(band_kernel, devices), out_shape=jax.Sha...  35.3 us
    unnamed x1, local copies, waits for them, and re-layouts  2.26 us

profile of v2, /device:TPU:0, one launch (start us, length us, event | category | flops | bytes accessed | tf_op | source)
XLA Modules:
  0.0 37.6 jit_solution(6728161895147826023)
XLA Ops:
  0.0 35.3 %shard_map.82 = f32[1,512,512]{2,1,0:T(8,128)} custom-call(f32[9,2,11]{2,1,0:T(2,128)} %bitcast.5, f32[5,3,4,9]{3,2,1,0:T(4,128)} %bitcast.4, f32[4,2,2,5]{3,2,1,0:T(2,128)} %bitcast.6, s32[16]{0:T(128)} %bitcast.7, s32[1,16]{1,0:T(1,128)} %slot_ref.1, s32[16]{0:T(128)} %owner_ref.1, bf16[4,5]{1,0:T(4,128)(2,1)} %weight_ref.1, f32[4,128,512]{2,1,0:T(8,128)} %image_ref.1), custom_call_target="tpu_custom_call" | custom-call | tf_op jit(solution)/shard_map/pallas_call | solution.py:448
  35.3 2.3 %copy.10 = f32[1,512,512]{2,1,0:T(8,128)} copy(f32[1,512,512]{2,1,0:T(8,128)} %shard_map.82) | data formatting | bytes 2097152

commit v3 on v2

--- a/solution.py
+++ b/solution.py
@@ -29,6 +29,7 @@
 HEIGHT = SPLIT * BLOCK
 LEFT = 16
 WINDOW = BLOCK + 2 * LEFT
+TILES = -(-3 * WINDOW // BLOCK)
 STEPS = 2 * REACH + 1
 COUNT = V * BLKC
 DEPTH = NBASIS * ROWS_IN
@@ -60,14 +61,6 @@
     return finish(sin_pi(offset) * sin_pi(offset / 3.0), offset)
 
 
-def outward(count):
-    far = sorted(range(1, count), key=lambda step: abs(step - count // 2))
-    half = len(far) // 2
-    near = far[half:][::-1]
-    mixed = [step for pair in zip(far[:half], near) for step in pair]
-    return mixed + near[half:]
-
-
 def split(values):
     high = values.astype(jnp.bfloat16)
     return high, (values - high.astype(jnp.float32)).astype(jnp.bfloat16)
@@ -79,6 +72,15 @@
 
 def band_kernel(
     devices,
+    taps_in,
+    coef_in,
+    affine_in,
+    patch_in,
+    slot_in,
+    owner_in,
+    weight_in,
+    image_ref,
+    out_ref,
     taps_ref,
     coef_ref,
     affine_ref,
@@ -86,8 +88,7 @@
     slot_ref,
     owner_ref,
     weight_ref,
-    image_ref,
-    out_ref,
+    loads,
     ext,
     col_kernel,
     lhs,
@@ -109,6 +110,32 @@
     band = lax.axis_index("ccd")
     barrier = pltpu.get_barrier_semaphore()
     sends = len(SENDS)
+    head, tail = FRESH[0][0], FRESH[0][0] + FRESH[0][1]
+    pieces = [
+        pltpu.make_async_copy(
+            image_ref.at[:, pl.ds(low - RIM, high - low)], ext.at[:, pl.ds(low, high - low)], own.at[sends + which]
+        )
+        for which, (low, high) in ((1, (head, tail)), (3, (RIM, head)), (4, (tail, RIM + BLOCK)))
+    ]
+    small = [
+        pltpu.make_async_copy(source, target, loads.at[which])
+        for which, (source, target) in enumerate(
+            (
+                (taps_in, taps_ref),
+                (owner_in, owner_ref),
+                (patch_in, patch_ref),
+                (slot_in, slot_ref),
+                (weight_in, weight_ref),
+                (affine_in, affine_ref),
+                (coef_in, coef_ref),
+            )
+        )
+    ]
+    pieces[0].start()
+    for copy in small:
+        copy.start()
+    for copy in pieces[1:]:
+        copy.start()
     for step in range(1, devices):
         pl.semaphore_signal(
             barrier,
@@ -116,9 +143,6 @@
             device_id={"ccd": lax.rem(band + step, devices)},
             device_id_type=pl.DeviceIdType.MESH,
         )
-    load = pltpu.make_async_copy(image_ref, ext.at[:, pl.ds(RIM, BLOCK)], own.at[sends + 1])
-    load.start()
-
     shifted = band + SPLIT // 2
     ccd = shifted // SPLIT
     top_row = shifted % SPLIT * BLOCK
@@ -131,41 +155,69 @@
         rows = first + lax.broadcasted_iota(jnp.int32, (count, 1), 0)
         return (rows >= region_low) & (rows < region_high)
 
-    weight_lane = lax.broadcasted_iota(jnp.int32, weight_ref.shape, 1)
-    weights = jnp.sum(
-        jnp.where(weight_lane == ccd, weight_ref[...].astype(jnp.float32), 0.0), axis=1, keepdims=True
-    )
-    owners = jnp.full((1, BLOCK), -1, jnp.int32)
-    cells = jnp.zeros((1, BLOCK), jnp.float32)
-    block_weight = jnp.zeros((1, BLOCK), jnp.float32)
-    for block in range(COUNT):
-        owners = jnp.where(lane == block, owner_ref[patch_ref[block]], owners)
-        cells = jnp.where(lane == block, slot_ref[0, block].astype(jnp.float32), cells)
-    for visit in range(V):
-        here = jnp.broadcast_to(weights[visit : visit + 1], (1, BLOCK))
-        block_weight = jnp.where(lane // BLKC == visit, here, block_weight)
-    lanes = lax.broadcasted_iota(jnp.int32, (devices, BLOCK), 1)
-    match = owners == lax.broadcasted_iota(jnp.int32, (devices, BLOCK), 0)
-    first = jnp.min(jnp.where(match, lanes, BLOCK), axis=1, keepdims=True)
-    last = jnp.max(jnp.where(match, lanes, -1), axis=1, keepdims=True)
-    is_first, is_last = lanes == first, lanes == last
-
-    def at(chosen, values):
-        return jnp.sum(jnp.where(chosen, values, 0.0), axis=1, keepdims=True)
-
-    note = jnp.where(
-        lanes < 2 * GROUP,
-        jnp.where(lanes < GROUP, at(is_first, cells), at(is_last, cells)),
-        jnp.where(
-            lanes < 3 * GROUP, at(is_first, block_weight), at(is_last & (last > first), block_weight)
-        ),
-    )
-    picks[...] = jnp.where(lanes == 0, jnp.where(last < 0, 0, first), jnp.maximum(last, 0))
-    to_plan = pltpu.make_async_copy(picks, plan, own.at[sends + 2])
-    to_plan.start()
-    for device in range(devices):
-        notes[device] = note[device : device + 1]
-
+    pad = jnp.zeros((ROWS_IN, TILES * BLOCK - 3 * WINDOW), jnp.bfloat16)
+
+    def fill(turn):
+        fresh, count = FRESH[turn]
+        for visit in range(V):
+            raw = ext[visit, fresh : fresh + count]
+            raw = jnp.where(inside(top_row + fresh - RIM, count), raw, 0.0)
+            side = jnp.zeros((count, LEFT), jnp.bfloat16)
+            high, low = (jnp.concatenate([side, part, side], axis=1) for part in split(raw))
+            for block in range(BLKC):
+                rows = slice((block * V + visit) * count, (block * V + visit + 1) * count)
+                window = slice(block * BLOCK, block * BLOCK + WINDOW)
+                row = jnp.concatenate([high[:, window], low[:, window], high[:, window], pad[:count]], axis=1)
+                for tile in range(TILES):
+                    lhs[tile, rows] = row[:, tile * BLOCK : (tile + 1) * BLOCK]
+
+    pieces[0].wait()
+    fill(0)
+    for copy in small:
+        copy.wait()
+
+    def make_plan():
+        weight_lane = lax.broadcasted_iota(jnp.int32, weight_ref.shape, 1)
+        weights = jnp.sum(
+            jnp.where(weight_lane == ccd, weight_ref[...].astype(jnp.float32), 0.0), axis=1, keepdims=True
+        )
+        owners = jnp.full((1, BLOCK), -1, jnp.int32)
+        cells = jnp.zeros((1, BLOCK), jnp.float32)
+        block_weight = jnp.zeros((1, BLOCK), jnp.float32)
+        for block in range(COUNT):
+            owners = jnp.where(lane == block, owner_ref[patch_ref[block]], owners)
+            cells = jnp.where(lane == block, slot_ref[0, block].astype(jnp.float32), cells)
+        for visit in range(V):
+            here = jnp.broadcast_to(weights[visit : visit + 1], (1, BLOCK))
+            block_weight = jnp.where(lane // BLKC == visit, here, block_weight)
+        lanes = lax.broadcasted_iota(jnp.int32, (devices, BLOCK), 1)
+        match = owners == lax.broadcasted_iota(jnp.int32, (devices, BLOCK), 0)
+        first = jnp.min(jnp.where(match, lanes, BLOCK), axis=1, keepdims=True)
+        last = jnp.max(jnp.where(match, lanes, -1), axis=1, keepdims=True)
+        is_first, is_last = lanes == first, lanes == last
+
+        def at(chosen, values):
+            return jnp.sum(jnp.where(chosen, values, 0.0), axis=1, keepdims=True)
+
+        note = jnp.where(
+            lanes < 2 * GROUP,
+            jnp.where(lanes < GROUP, at(is_first, cells), at(is_last, cells)),
+            jnp.where(
+                lanes < 3 * GROUP, at(is_first, block_weight), at(is_last & (last > first), block_weight)
+            ),
+        )
+        picks[...] = jnp.where(lanes == 0, jnp.where(last < 0, 0, first), jnp.maximum(last, 0))
+        to_plan = pltpu.make_async_copy(picks, plan, own.at[sends + 2])
+        to_plan.start()
+        for device in range(devices):
+            notes[device] = note[device : device + 1]
+
+        return to_plan
+
+    for basis in range(NBASIS):
+        col_kernel[basis, 3 * WINDOW : TILES * BLOCK] = jnp.zeros(
+            (TILES * BLOCK - 3 * WINDOW, BLOCK), jnp.bfloat16
+        )
     sub = lax.broadcasted_iota(jnp.int32, (8, BLOCK), 0)
     across = lax.broadcasted_iota(jnp.int32, (8, BLOCK), 1)
     edge = LEFT - HALF
@@ -176,7 +228,6 @@
         taps = pltpu.roll(taps, 0, 1, stride=1, stride_axis=0)
         high = taps.astype(jnp.bfloat16).astype(jnp.float32)
         low = taps - high
-        cols = slice(basis * BLOCK, (basis + 1) * BLOCK)
         for part, offsets in ((high, (0, WINDOW)), (low, (2 * WINDOW,))):
             rows = []
             for group in range(WINDOW // 8):
@@ -185,7 +236,7 @@
                 rows.append(jnp.where((tap >= 0) & (tap < TAPS), turned, 0.0))
             matrix = jnp.concatenate(rows, axis=0).astype(jnp.bfloat16)
             for offset in offsets:
-                col_kernel[offset : offset + WINDOW, cols] = matrix
+                col_kernel[basis, offset : offset + WINDOW] = matrix
 
     wide_lane = lax.broadcasted_iota(jnp.int32, (1, DEPTH), 1)
     starts = [wide_lane >= basis * ROWS_IN for basis in range(NBASIS)]
@@ -267,7 +318,6 @@
             device_id_type=pl.DeviceIdType.MESH,
         )
 
-    load.wait()
     batches = []
     for turn, chunk in enumerate(ORDER):
         if chunk == 0:
@@ -281,30 +331,28 @@
                 to_last().wait_send()
                 to_next().wait_recv()
 
+        if turn == 1:
+            for copy in pieces[1:]:
+                copy.wait()
+
         fresh, count = FRESH[turn]
-        for visit in range(V):
-            raw = ext[visit, fresh : fresh + count]
-            raw = jnp.where(inside(top_row + fresh - RIM, count), raw, 0.0)
-            side = jnp.zeros((count, LEFT), jnp.bfloat16)
-            high, low = (jnp.concatenate([side, part, side], axis=1) for part in split(raw))
-            for block in range(BLKC):
-                rows = slice((block * V + visit) * count, (block * V + visit + 1) * count)
-                window = slice(block * BLOCK, block * BLOCK + WINDOW)
-                lhs[rows, 0:WINDOW] = high[:, window]
-                lhs[rows, WINDOW : 2 * WINDOW] = low[:, window]
-                lhs[rows, 2 * WINDOW : 3 * WINDOW] = high[:, window]
+        if turn > 0:
+            fill(turn)
         for pair in range(0, NBASIS, 2):
             bases = range(pair, min(pair + 2, NBASIS))
-            cols = slice(pair * BLOCK, (bases[-1] + 1) * BLOCK)
-            high, low = split(dot(lhs[0 : COUNT * count, :], col_kernel[:, cols]))
+            left = jnp.concatenate([lhs[tile, 0 : COUNT * count] for tile in range(TILES)], axis=1)
+            right = jnp.concatenate([col_kernel[basis] for basis in bases], axis=1)
+            high, low = split(dot(left, right))
             for block in range(BLKC):
                 for visit in range(V):
                     rows = slice((block * V + visit) * count, (block * V + visit + 1) * count)
                     for basis in bases:
                         part = slice((basis - pair) * BLOCK, (basis - pair + 1) * BLOCK)
-                        into = slice(fresh, fresh + count), slice(block * BLOCK, (block + 1) * BLOCK)
-                        terms_high[visit, basis, into[0], into[1]] = high[rows, part]
-                        terms_low[visit, basis, into[0], into[1]] = low[rows, part]
+                        terms_high[visit, block, basis, fresh : fresh + count] = high[rows, part]
+                        terms_low[visit, block, basis, fresh : fresh + count] = low[rows, part]
+
+        if turn == 0:
+            to_plan = make_plan()
 
         top = top_row + chunk * CHUNK
         own_rows = (top + lax.broadcasted_iota(jnp.int32, (CHUNK, 1), 0)).astype(jnp.float32)
@@ -320,10 +368,14 @@
             level = row_kernel * (constant + by_row * row_pos)
             high, low = split(jnp.concatenate([level, row_kernel * by_column], axis=0))
             rows = slice(chunk * CHUNK, chunk * CHUNK + ROWS_IN)
-            upper = dot(
-                jnp.concatenate([high, low], axis=0), terms_high[visit, :, rows, :].reshape(DEPTH, WIDTH)
+            right_high, right_low = (
+                jnp.concatenate(
+                    [part[visit, block, :, rows, :].reshape(DEPTH, BLOCK) for block in range(BLKC)], axis=1
+                )
+                for part in (terms_high, terms_low)
             )
-            lower = dot(high, terms_low[visit, :, rows, :].reshape(DEPTH, WIDTH))
+            upper = dot(jnp.concatenate([high, low], axis=0), right_high)
+            lower = dot(high, right_low)
             both = upper[: 2 * ROWS_MID] + upper[2 * ROWS_MID :] + lower
             matched = both[:ROWS_MID] + both[ROWS_MID:] * col_pos
             mid[visit] = jnp.where(keep, matched, 0.0)
@@ -364,7 +416,7 @@
                 continue
             rows = pl.ds(turns[0] * CHUNK, len(turns) * CHUNK)
             batch = []
-            for step in outward(devices):
+            for step in range(1, devices):
                 target = lax.rem(band + step, devices)
                 batch.append(
                     remote(outbox.at[target, :, rows], inbox.at[band, :, rows], send, step)
@@ -377,7 +429,7 @@
             batches.append(batch)
         if turn == 0:
             batch = []
-            for step in outward(devices):
+            for step in range(1, devices):
                 batch.append(
                     remote(notes.at[lax.rem(band + step, devices)], table.at[band], sends, step)
                 )
@@ -440,7 +492,15 @@
     images, basis_taps, psf_coef, affine, visit_weight, block_patch, block_slot, patch_owner
 ):
     devices = lax.axis_size("ccd")
-    scalars = pl.BlockSpec(memory_space=pltpu.SMEM)
+    small = (
+        basis_taps.transpose(1, 0, 2),
+        psf_coef.transpose(1, 3, 0, 2),
+        affine.transpose(0, 2, 3, 1),
+        block_patch.reshape(-1),
+        block_slot,
+        patch_owner,
+        visit_weight,
+    )
     vector = pl.BlockSpec(memory_space=pltpu.VMEM)
     sends = len(SENDS)
     half = jnp.bfloat16
@@ -448,14 +508,17 @@
     return pl.pallas_call(
         functools.partial(band_kernel, devices),
         out_shape=jax.ShapeDtypeStruct((1, size, size), jnp.float32),
-        in_specs=[scalars] * 6 + [vector, pl.BlockSpec(memory_space=pl.ANY)],
+        in_specs=[pl.BlockSpec(memory_space=pltpu.HBM)] * (len(small) + 1),
         out_specs=vector,
-        scratch_shapes=[
+        scratch_shapes=[pltpu.SMEM(array.shape, array.dtype) for array in small[:-1]]
+        + [
+            pltpu.VMEM(visit_weight.shape, half),
+            pltpu.SemaphoreType.DMA((len(small),)),
             pltpu.VMEM((V, EXT, WIDTH), jnp.float32),
-            pltpu.VMEM((3 * WINDOW, NBASIS * BLOCK), half),
-            pltpu.VMEM((COUNT * ROWS_IN, 3 * WINDOW), half),
-            pltpu.VMEM((V, NBASIS, EXT, WIDTH), half),
-            pltpu.VMEM((V, NBASIS, EXT, WIDTH), half),
+            pltpu.VMEM((NBASIS, TILES * BLOCK, BLOCK), half),
+            pltpu.VMEM((TILES, COUNT * ROWS_IN, BLOCK), half),
+            pltpu.VMEM((V, BLKC, NBASIS, EXT, BLOCK), half),
+            pltpu.VMEM((V, BLKC, NBASIS, EXT, BLOCK), half),
             pltpu.VMEM((V, ROWS_MID, WIDTH), jnp.float32),
             pltpu.VMEM((len(ORDER), COUNT, CHUNK, BLOCK), half),
             pltpu.VMEM((devices, CAP, BLOCK, BLOCK), half),
@@ -466,20 +529,11 @@
             pltpu.SMEM((devices, BLOCK), jnp.int32),
             pltpu.SemaphoreType.DMA((sends + 1, devices)),
             pltpu.SemaphoreType.DMA((sends + 1, devices)),
-            pltpu.SemaphoreType.DMA((sends + 3,)),
+            pltpu.SemaphoreType.DMA((sends + 5,)),
             pltpu.SemaphoreType.DMA((4,)),
         ],
-        compiler_params=pltpu.CompilerParams(collective_id=1, has_side_effects=True),
-    )(
-        basis_taps.transpose(1, 0, 2),
-        psf_coef.transpose(1, 3, 0, 2),
-        affine.transpose(0, 2, 3, 1),
-        block_patch.reshape(-1),
-        block_slot,
-        patch_owner,
-        visit_weight,
-        images,
-    )
+        compiler_params=pltpu.CompilerParams(collective_id=1, has_side_effects=True, vmem_limit_bytes=40 << 20),
+    )(*(pltpu.with_memory_space_constraint(array, pltpu.HBM) for array in (*small, images)))
 
 
 def solution(mesh):

time: 37.9 us -> 33.3 us (0.88)
  the two profiles are of different devices: /device:TPU:0 before, /device:TPU:15 now
where the time goes in v3:
time: 33.3 us; the launch traced here: 33.1 us
  Pallas kernels  32.2 us (97%)
  local copies, waits for them, and re-layouts  0.97 us (3%)
    pallas_call x1, Pallas kernels, shards(): pl.pallas_call(functools.partial(band_kernel, devices), out_shape=jax.Sha...  32.2 us
    unnamed x1, local copies, waits for them, and re-layouts  0.97 us

profile of v3, /device:TPU:15, one launch (start us, length us, event | category | flops | bytes accessed | tf_op | source)
XLA Modules:
  0.0 33.1 jit_solution(6913168148644500208)
XLA Ops:
  0.0 32.2 %shard_map.82 = f32[1,512,512]{2,1,0:T(8,128)S(1)} custom-call(f32[9,2,11]{2,1,0:T(2,128)} %bitcast.5, f32[5,3,4,9]{3,2,1,0:T(4,128)} %bitcast.4, f32[4,2,2,5]{3,2,1,0:T(2,128)} %bitcast.6, s32[16]{0:T(128)} %bitcast.7, s32[1,16]{1,0:T(1,128)} %slot_in.1, s32[16]{0:T(128)} %owner_in.1, bf16[4,5]{1,0:T(4,128)(2,1)} %weight_in.1, f32[4,128,512]{2,1,0:T(8,128)} %image_ref.1), custom_call_target="tpu_custom_call" | custom-call | tf_op jit(solution)/shard_map/pallas_call | solution.py:508
  32.2 1.0 %copy.10 = f32[1,512,512]{2,1,0:T(8,128)} copy(f32[1,512,512]{2,1,0:T(8,128)S(1)} %shard_map.82) | data formatting | bytes 2097152

commit v4 on v3

--- a/solution.py
+++ b/solution.py
@@ -19,12 +19,9 @@
 HALF = TAPS // 2
 REACH = 3
 RIM = HALF + REACH
-CHUNK = 32
 CAP = 2
 GROUP = 16
 EXT = BLOCK + 2 * RIM
-ROWS_IN = CHUNK + 2 * RIM
-ROWS_MID = CHUNK + 8
 WIDTH = BLKC * BLOCK
 HEIGHT = SPLIT * BLOCK
 LEFT = 16
@@ -32,9 +29,11 @@
 TILES = -(-3 * WINDOW // BLOCK)
 STEPS = 2 * REACH + 1
 COUNT = V * BLKC
-DEPTH = NBASIS * ROWS_IN
-ORDER = (1, 2, 0, 3)
-FRESH = ((32, 48), (80, 32), (0, 32), (112, 32))
+TURNS = ((48, 16, 48, 32), (64, 48, 80, 48), (0, 48, 0, 48), (112, 16, 128, 16))
+OFFSETS = tuple(sum(turn[1] for turn in TURNS[:index]) for index in range(len(TURNS)))
+MOST = max(turn[1] for turn in TURNS)
+FRESH = tuple(turn[2:] for turn in TURNS)
+LINES = max(turn[3] for turn in TURNS)
 SENDS = ((0,), (1,), (2, 3))
 SINE = [(-1) ** k * math.pi ** (2 * k + 1) / math.factorial(2 * k + 1) for k in range(7)]
 
@@ -155,7 +154,7 @@
         rows = first + lax.broadcasted_iota(jnp.int32, (count, 1), 0)
         return (rows >= region_low) & (rows < region_high)
 
-    pad = jnp.zeros((ROWS_IN, TILES * BLOCK - 3 * WINDOW), jnp.bfloat16)
+    pad = jnp.zeros((LINES, TILES * BLOCK - 3 * WINDOW), jnp.bfloat16)
 
     def fill(turn):
         fresh, count = FRESH[turn]
@@ -231,29 +230,41 @@
         for part, offsets in ((high, (0, WINDOW)), (low, (2 * WINDOW,))):
             rows = []
             for group in range(WINDOW // 8):
-                turned = pltpu.roll(part, group * 8 % BLOCK, 1) if group * 8 % BLOCK else part
-                tap = group * 8 + sub - edge - across
-                rows.append(jnp.where((tap >= 0) & (tap < TAPS), turned, 0.0))
+                top = group * 8
+                if top + 7 < edge or top - edge - TAPS + 1 > BLOCK - 1:
+                    rows.append(jnp.zeros((8, BLOCK), jnp.float32))
+                    continue
+                turned = pltpu.roll(part, top % BLOCK, 1) if top % BLOCK else part
+                if top - edge - TAPS + 1 < 0 or top + 7 - edge > BLOCK - 1:
+                    tap = top + sub - edge - across
+                    turned = jnp.where((tap >= 0) & (tap < TAPS), turned, 0.0)
+                rows.append(turned)
             matrix = jnp.concatenate(rows, axis=0).astype(jnp.bfloat16)
             for offset in offsets:
                 col_kernel[basis, offset : offset + WINDOW] = matrix
 
-    wide_lane = lax.broadcasted_iota(jnp.int32, (1, DEPTH), 1)
-    starts = [wide_lane >= basis * ROWS_IN for basis in range(NBASIS)]
-
-    def by_basis(value):
-        total = jnp.full((1, DEPTH), value(0), jnp.float32)
+    def row_band(count):
+        rows_in, rows_mid = count + 2 * RIM, count + 8
+        depth = NBASIS * rows_in
+        wide_lane = lax.broadcasted_iota(jnp.int32, (1, depth), 1)
+        starts = [wide_lane >= basis * rows_in for basis in range(NBASIS)]
+
+        def by_basis(value):
+            total = jnp.full((1, depth), value(0), jnp.float32)
+            for basis in range(1, NBASIS):
+                total = jnp.where(starts[basis], value(basis), total)
+            return total
+
+        start = jnp.zeros((1, depth), jnp.int32)
         for basis in range(1, NBASIS):
-            total = jnp.where(starts[basis], value(basis), total)
-        return total
-
-    start = jnp.zeros((1, DEPTH), jnp.int32)
-    for basis in range(1, NBASIS):
-        start = jnp.where(starts[basis], basis * ROWS_IN, start)
-    gap = (wide_lane - start) - lax.broadcasted_iota(jnp.int32, (ROWS_MID, DEPTH), 0)
-    row_kernel = jnp.zeros(gap.shape, jnp.float32)
-    for tap in range(TAPS):
-        row_kernel = jnp.where(gap == tap, by_basis(lambda basis: taps_ref[basis, 0, tap]), row_kernel)
+            start = jnp.where(starts[basis], basis * rows_in, start)
+        gap = (wide_lane - start) - lax.broadcasted_iota(jnp.int32, (rows_mid, depth), 0)
+        row_kernel = jnp.zeros(gap.shape, jnp.float32)
+        for tap in range(TAPS):
+            row_kernel = jnp.where(gap == tap, by_basis(lambda basis: taps_ref[basis, 0, tap]), row_kernel)
+        return row_kernel, by_basis
+
+    bands = {TURNS[0][1]: row_band(TURNS[0][1])}
 
     column = lax.broadcasted_iota(jnp.int32, (1, WIDTH), 1).astype(jnp.float32)
     col_pos = (2.0 * column + 1.0) / WIDTH - 1.0
@@ -319,8 +330,8 @@
         )
 
     batches = []
-    for turn, chunk in enumerate(ORDER):
-        if chunk == 0:
+    for turn, (begin, size, _, _) in enumerate(TURNS):
+        if turn == 2:
             @pl.when(has_next)
             def _():
                 to_next().wait_send()
@@ -354,52 +365,57 @@
         if turn == 0:
             to_plan = make_plan()
 
-        top = top_row + chunk * CHUNK
-        own_rows = (top + lax.broadcasted_iota(jnp.int32, (CHUNK, 1), 0)).astype(jnp.float32)
+        if size not in bands:
+            bands[size] = row_band(size)
+        row_kernel, by_basis = bands[size]
+        rows_in, rows_mid = size + 2 * RIM, size + 8
+        depth = NBASIS * rows_in
+        top = top_row + begin
+        own_rows = (top + lax.broadcasted_iota(jnp.int32, (size, 1), 0)).astype(jnp.float32)
         row_shift = row_base + row_slope * ((own_rows - (HEIGHT - 1) / 2.0) / HEIGHT)
         row_weight = lanczos(row_shift - row_step)
-        position = (top - REACH + lax.broadcasted_iota(jnp.int32, (ROWS_MID, 1), 0)).astype(jnp.float32)
+        position = (top - REACH + lax.broadcasted_iota(jnp.int32, (rows_mid, 1), 0)).astype(jnp.float32)
         row_pos = (2.0 * position + 1.0) / HEIGHT - 1.0
-        keep = inside(top - REACH, ROWS_MID)
+        keep = inside(top - REACH, rows_mid)
         for visit in range(V):
             constant, by_row, by_column = (
                 by_basis(lambda basis: coef_ref[ccd, part, visit, basis]) for part in range(3)
             )
             level = row_kernel * (constant + by_row * row_pos)
             high, low = split(jnp.concatenate([level, row_kernel * by_column], axis=0))
-            rows = slice(chunk * CHUNK, chunk * CHUNK + ROWS_IN)
+            rows = slice(begin, begin + rows_in)
             right_high, right_low = (
                 jnp.concatenate(
-                    [part[visit, block, :, rows, :].reshape(DEPTH, BLOCK) for block in range(BLKC)], axis=1
+                    [part[visit, block, :, rows, :].reshape(depth, BLOCK) for block in range(BLKC)], axis=1
                 )
                 for part in (terms_high, terms_low)
             )
             upper = dot(jnp.concatenate([high, low], axis=0), right_high)
             lower = dot(high, right_low)
-            both = upper[: 2 * ROWS_MID] + upper[2 * ROWS_MID :] + lower
-            matched = both[:ROWS_MID] + both[ROWS_MID:] * col_pos
-            mid[visit] = jnp.where(keep, matched, 0.0)
-
-            warped = jnp.zeros((CHUNK, WIDTH), jnp.float32)
+            both = upper[: 2 * rows_mid] + upper[2 * rows_mid :] + lower
+            matched = both[:rows_mid] + both[rows_mid:] * col_pos
+            mid[visit, 0:rows_mid] = jnp.where(keep, matched, 0.0)
+
+            warped = jnp.zeros((size, WIDTH), jnp.float32)
             for step in range(STEPS):
                 column_of = visit * 8 + step
-                warped = warped + row_weight[:, column_of : column_of + 1] * mid[visit, step : step + CHUNK, :]
-            total = jnp.zeros((CHUNK, WIDTH), jnp.float32)
+                warped = warped + row_weight[:, column_of : column_of + 1] * mid[visit, step : step + size, :]
+            total = jnp.zeros((size, WIDTH), jnp.float32)
             for step in range(STEPS):
                 offset = step - REACH
                 moved = warped if offset == 0 else pltpu.roll(warped, (-offset) % WIDTH, 1)
                 total = total + col_weight[visit][step : step + 1, :] * moved
             rounded = total.astype(jnp.bfloat16)
             for block in range(BLKC):
-                stage[turn, visit * BLKC + block] = rounded[:, block * BLOCK : (block + 1) * BLOCK]
+                stage[turn, visit * BLKC + block, 0:size] = rounded[:, block * BLOCK : (block + 1) * BLOCK]
 
         if turn == 0:
             to_plan.wait()
-        rows = slice(turn * CHUNK, (turn + 1) * CHUNK)
+        rows = slice(OFFSETS[turn], OFFSETS[turn] + size)
         for device in range(devices):
             for slot in range(CAP):
                 pick = jnp.minimum(jnp.maximum(plan[device, slot], 0), COUNT - 1)
-                outbox[device, slot, rows] = stage[turn, pick]
+                outbox[device, slot, rows] = stage[turn, pick, 0:size]
         if turn == 0:
             pl.semaphore_wait(barrier, devices - 1)
 
@@ -414,7 +430,7 @@
         for send, turns in enumerate(SENDS):
             if turns[-1] != turn:
                 continue
-            rows = pl.ds(turns[0] * CHUNK, len(turns) * CHUNK)
+            rows = pl.ds(OFFSETS[turns[0]], sum(TURNS[each][1] for each in turns))
             batch = []
             for step in range(1, devices):
                 target = lax.rem(band + step, devices)
@@ -472,14 +488,14 @@
         for copy in batch:
             copy.wait()
         for turn in turns:
-            groups = range(turn * CHUNK, (turn + 1) * CHUNK, GROUP)
+            groups = range(OFFSETS[turn], OFFSETS[turn] + TURNS[turn][1], GROUP)
             blocks = jnp.concatenate(
                 [inbox[:, :, group : group + GROUP, :].reshape(span, BLOCK) for group in groups], axis=1
             )
             result = dot(mixing, blocks)
             for index, group in enumerate(groups):
                 part = result[:, index * BLOCK : (index + 1) * BLOCK] * scale
-                row = ORDER[turn] * CHUNK + index * GROUP
+                row = TURNS[turn][0] + index * GROUP
                 for cell in range(CELLS):
                     out_ref[
                         0,
@@ -516,11 +532,11 @@
             pltpu.SemaphoreType.DMA((len(small),)),
             pltpu.VMEM((V, EXT, WIDTH), jnp.float32),
             pltpu.VMEM((NBASIS, TILES * BLOCK, BLOCK), half),
-            pltpu.VMEM((TILES, COUNT * ROWS_IN, BLOCK), half),
+            pltpu.VMEM((TILES, COUNT * LINES, BLOCK), half),
             pltpu.VMEM((V, BLKC, NBASIS, EXT, BLOCK), half),
             pltpu.VMEM((V, BLKC, NBASIS, EXT, BLOCK), half),
-            pltpu.VMEM((V, ROWS_MID, WIDTH), jnp.float32),
-            pltpu.VMEM((len(ORDER), COUNT, CHUNK, BLOCK), half),
+            pltpu.VMEM((V, MOST + 8, WIDTH), jnp.float32),
+            pltpu.VMEM((len(TURNS), COUNT, MOST, BLOCK), half),
             pltpu.VMEM((devices, CAP, BLOCK, BLOCK), half),
             pltpu.VMEM((devices, CAP, BLOCK, BLOCK), half),
             pltpu.VMEM((devices, 1, BLOCK), jnp.float32),

time: 33.3 us -> 32.8 us (0.985)
  the two profiles are of different devices: /device:TPU:15 before, /device:TPU:13 now
where the time goes in v4:
time: 32.8 us; the launch traced here: 32.7 us
  Pallas kernels  31.7 us (97%)
  local copies, waits for them, and re-layouts  0.97 us (3%)
    pallas_call x1, Pallas kernels, shards(): pl.pallas_call(functools.partial(band_kernel, devices), out_shape=jax.Sha...  31.7 us
    unnamed x1, local copies, waits for them, and re-layouts  0.97 us

profile of v4, /device:TPU:13, one launch (start us, length us, event | category | flops | bytes accessed | tf_op | source)
XLA Modules:
  0.0 32.7 jit_solution(17634467411927207463)
XLA Ops:
  0.0 31.7 %shard_map.82 = f32[1,512,512]{2,1,0:T(8,128)S(1)} custom-call(f32[9,2,11]{2,1,0:T(2,128)} %bitcast.5, f32[5,3,4,9]{3,2,1,0:T(4,128)} %bitcast.4, f32[4,2,2,5]{3,2,1,0:T(2,128)} %bitcast.6, s32[16]{0:T(128)} %bitcast.7, s32[1,16]{1,0:T(1,128)} %slot_in.1, s32[16]{0:T(128)} %owner_in.1, bf16[4,5]{1,0:T(4,128)(2,1)} %weight_in.1, f32[4,128,512]{2,1,0:T(8,128)} %image_ref.1), custom_call_target="tpu_custom_call" | custom-call | tf_op jit(solution)/shard_map/pallas_call | solution.py:524
  31.7 1.0 %copy.10 = f32[1,512,512]{2,1,0:T(8,128)} copy(f32[1,512,512]{2,1,0:T(8,128)S(1)} %shard_map.82) | data formatting | bytes 2097152
